TPU v7x, 128 devices: a whole 4x4x4 slice. The times are simulated.
128 devices in a mesh: gx: 16 (over x, z_lo, core), gy: 8 (over z_hi, y).
Axes of the slice: x: 4, y: 4, z: 4 (z_hi: 2, z_lo: 2; z = z_hi * 2 + z_lo), core: 2. Of those that a mesh axis runs over, the one named last changes fastest.
Arguments:
- density: float32 [512, 1024, 256], P('gx', 'gy'), as said below
- reaction_rates: float32 [6], replicated, may hold values from 0.3 to 3
- state_changes: int32 [6, 3], replicated, may hold values from -2 to 2, as said below
- target_box: int32 [2, 3], replicated, may hold values from 0 to 1024, as said below
- truncation: int32 [2], replicated, may hold values from 5 to 16
Outputs:
- occupancy: float32 [512, 1024, 256], P('gx', 'gy')
- summary: float32 [2], replicated
Inputs may be any that keep to these rules, and one draw needn't show every extreme that they name: density is positive. `state_changes`: each row is one reaction's change of the three counts; for each of the first two species, some reaction changes it by 2 and some by -2. For each species, target_box[0, d] < target_box[1, d], and target_box[1, d] is at most that species' number of counts; along the species with the most counts the box reaches the lattice's end.
All inputs are finite; a program needn't handle non-finite values.
Results may differ from a plain program's by a relative error of at most 0.0001.
Values sent between devices are 32-bit elements; how exact they have to be, the bound alone decides.
A program may use at most 256 MiB of HBM per device.

v0:
```python
import math

import jax
import jax.numpy as jnp
from jax import lax
from jax.sharding import PartitionSpec as P

STEPS = 4


mean_jumps = 8.0
headroom = 1.05
series_length = 40


def extended_2(cells, sides, width):
    for axis, dim in sides:
        count = lax.axis_size(axis)
        ends = count - 1
        head = lax.slice_in_dim(cells, 0, width, axis=dim)
        tail = lax.slice_in_dim(cells, cells.shape[dim] - width, cells.shape[dim], axis=dim)
        cells = jnp.concatenate(
            [
                lax.ppermute(tail, axis, [(i, (i + 1) % count) for i in range(ends)]),
                cells,
                lax.ppermute(head, axis, [((i + 1) % count, i) for i in range(ends)]),
            ],
            axis=dim,
        )
    return cells


def propensity_factor(counts, reactant_order, extent):
    values = counts.astype(jnp.float32)
    linear = values / extent
    square = values * (values - 1.0) / (extent * extent)
    return jnp.where(
        reactant_order == 0, jnp.ones_like(values), jnp.where(reactant_order == 1, linear, square)
    )


def box_indicator(counts, target_box, axis_number):
    return ((counts >= target_box[0, axis_number]) & (counts < target_box[1, axis_number])).astype(
        jnp.float32
    )


def outer_three(along_first, along_second, along_third):
    return along_first[:, None, None] * along_second[None, :, None] * along_third[None, None, :]


def jump_weights(truncation):
    table = [
        math.exp(-mean_jumps) * mean_jumps**jump_index / math.factorial(jump_index)
        for jump_index in range(series_length)
    ]
    weights = [jnp.float32(table[jump_index]) for jump_index in range(STEPS + 1)]
    tails = []
    for which in range(2):
        tail_weight = jnp.float32(0.0)
        for jump_index in range(STEPS + 1, series_length):
            taken = (jump_index <= truncation[which]).astype(jnp.float32)
            tail_weight = tail_weight + taken * jnp.float32(table[jump_index])
        tails.append(tail_weight)
    return (weights, tails[0], tails[1])


def body(density, reaction_rates, state_changes, target_box, truncation):
    block_first, block_second, species_third = density.shape
    extent_first = block_first * lax.axis_size("gx")
    extent_second = block_second * lax.axis_size("gy")
    anchor_first = lax.axis_index("gx") * block_first
    anchor_second = lax.axis_index("gy") * block_second
    extents = (extent_first, extent_second, species_third)
    reactant_orders = jnp.maximum(-state_changes, 0)
    reaction_total = state_changes.shape[0]
    corner = None
    for reaction in range(reaction_total):
        corner_term = reaction_rates[reaction]
        for axis_number in range(3):
            last_count = jnp.full((1,), extents[axis_number] - 1, jnp.int32)
            corner_term = (
                corner_term
                * propensity_factor(
                    last_count, reactant_orders[reaction, axis_number], float(extents[axis_number])
                )[0]
            )
        corner = corner_term if corner is None else corner + corner_term
    uniform_rate = headroom * corner

    def advance(extended, margin):
        length_first = extended.shape[0]
        length_second = extended.shape[1]
        counts_first = anchor_first - margin + jnp.arange(length_first, dtype=jnp.int32)
        counts_second = anchor_second - margin + jnp.arange(length_second, dtype=jnp.int32)
        counts_third = jnp.arange(-2, species_third + 2, dtype=jnp.int32)
        count_grids = (counts_first, counts_second, counts_third)
        free = 1.0 - outer_three(
            box_indicator(counts_first, target_box, 0),
            box_indicator(counts_second, target_box, 1),
            box_indicator(counts_third, target_box, 2),
        )
        padded = jnp.pad(extended, ((0, 0), (0, 0), (2, 2)))
        scaled = padded * free / uniform_rate
        coefficients = []
        for reaction in range(reaction_total):
            factors = [
                propensity_factor(
                    count_grids[axis_number],
                    reactant_orders[reaction, axis_number],
                    float(extents[axis_number]),
                )
                for axis_number in range(3)
            ]
            coefficients.append(
                outer_three(reaction_rates[reaction] * factors[0], factors[1], factors[2])
            )
        total_rate = coefficients[0]
        for reaction in range(1, reaction_total):
            total_rate = total_rate + coefficients[reaction]
        advanced = extended[2:-2, 2:-2, :] - total_rate[2:-2, 2:-2, 2:-2] * scaled[2:-2, 2:-2, 2:-2]
        for reaction in range(reaction_total):
            flux_term = scaled * coefficients[reaction]
            start = [2 - state_changes[reaction, axis_number] for axis_number in range(3)]
            arrival = lax.dynamic_slice(
                flux_term, start, (length_first - 4, length_second - 4, species_third)
            )
            advanced = advanced + arrival
        return advanced

    interior_box = outer_three(
        box_indicator(anchor_first + jnp.arange(block_first, dtype=jnp.int32), target_box, 0),
        box_indicator(anchor_second + jnp.arange(block_second, dtype=jnp.int32), target_box, 1),
        box_indicator(jnp.arange(species_third, dtype=jnp.int32), target_box, 2),
    )
    mass_sums = []
    hit_sums = []

    def record(current):
        local_sums = (jnp.sum(current), jnp.sum(current * interior_box))
        local_sums = lax.psum((local_sums[0], local_sums[1]), ("gx", "gy"))
        mass_sums.append(local_sums[0])
        hit_sums.append(local_sums[1])

    weights, tail_density, tail_totals = jump_weights(truncation)
    current = density
    record(current)
    accumulated = weights[0] * density
    for jump_index in range(1, STEPS + 1):
        extended = extended_2(current, (("gx", 0), ("gy", 1)), 2)
        current = advance(extended, 2)
        record(current)
        accumulated = accumulated + weights[jump_index] * current
    occupancy = accumulated + tail_density * current
    reached = weights[0] * hit_sums[0]
    retained = weights[0] * mass_sums[0]
    for jump_index in range(1, STEPS + 1):
        reached = reached + weights[jump_index] * hit_sums[jump_index]
        retained = retained + weights[jump_index] * mass_sums[jump_index]
    cell_total = float(extent_first * extent_second * species_third)
    reached = (reached + tail_totals * hit_sums[STEPS]) / cell_total
    retained = (retained + tail_totals * mass_sums[STEPS]) / cell_total
    return (occupancy, jnp.stack([reached, retained]))


def solution(mesh):
    placed = (P("gx", "gy", None), P(), P(), P(), P())
    return jax.shard_map(
        body, mesh=mesh, in_specs=placed, out_specs=(P("gx", "gy", None), P()), check_vma=False
    )
```

profile of v0, /device:TPU:1, one launch (start us, length us, event | category | flops | bytes accessed | tf_op | source)
XLA Modules:
  0.0 492.3 jit_solution(11451059432423946382)
XLA Ops:
  1.7 4.9 %collective-permute-start = (f32[2,128,256]{2,1,0:T(8,128)S(1)}, f32[2,128,256]{2,1,0:T(8,128)S(1)}, u32[]{:S(2)}, u32[]{:S(2)}) collective-permute-start(f32[2,128,256]{2,1,0:T(8,128)S(1)} %get-tuple-element.48), channel_id=1, source_target_pairs={{0,8},{8,16},{16,24},{24,32},{32,40},{40,48},{48,56},{56,64},{64,7... | collective-permute-start | bytes 786440 | tf_op jit(solution)/shard_map/ppermute | solution.py:24
  6.6 1.9 collective-permute-start.1
  32.1 2.1 fusion.61
  34.2 1.5 fusion.65
  35.7 1.5 fusion.63
  37.3 1.3 and_convert_fusion.3
  38.6 1.3 fusion.53
  40.0 3.4 broadcast_multiply_fusion
  43.6 3.5 broadcast_multiply_fusion.1
  48.3 3.5 broadcast_multiply_fusion.2
  51.8 3.5 broadcast_multiply_fusion.3
  56.7 3.5 broadcast_multiply_fusion.4
  60.3 3.4 broadcast_multiply_fusion.5
  63.7 1.3 and_convert_fusion.4
  91.3 3.1 constant_dynamic-update-slice_fusion.1
  94.5 3.2 collective-permute-start.2
  97.7 1.3 collective-permute-start.3
  100.2 2.7 collective-permute-done.3
  102.8 4.5 fusion.7
  107.4 31.3 %fusion.35 = (f32[32,128,256]{2,1,0:T(8,128)S(1)}, f32[32,128,256]{2,1,0:T(8,128)}) fusion(f32[36,132,260]{2,1,0:T(8,128)S(1)} %fusion.7, s32[]{:T(128)S(6)} %select_n.1085, s32[]{:T(128)S(6)} %select_n.1086, s32[]{:T(128)S(6)} %select_n.1087, s32[]{:T(128)S(6)} %select_n.1082, s32[]{:T(128)S(6)} %select_n.1083, s32[]{:T(128)S(6)} %select_n.1084, ...), kind=kLoop, calls=%fused_computation.79 | loop fusion | flops 19922944 | bytes 92274760 | tf_op jit(solution)/shard_map/add | solution.py:128
  138.7 5.1 %collective-permute-start.4 = (f32[2,128,256]{2,1,0:T(8,128)S(1)}, f32[2,128,256]{2,1,0:T(8,128)S(1)}, u32[]{:S(2)}, u32[]{:S(2)}) collective-permute-start(f32[2,128,256]{2,1,0:T(8,128)S(1)} %get-tuple-element.45), channel_id=1, source_target_pairs={{0,8},{8,16},{16,24},{24,32},{32,40},{40,48},{48,56},{56,64},{64,7... | collective-permute-start | bytes 786440 | tf_op jit(solution)/shard_map/ppermute | solution.py:24
  143.8 1.9 collective-permute-start.5
  145.7 1.4 collective-permute-done.4
  147.1 4.4 collective-permute-done.5
  151.6 3.2 collective-permute-start.6
  154.8 1.5 collective-permute-start.7
  156.3 3.8 collective-permute-done.7
  160.1 8.8 %fusion.5 = f32[36,132,260]{2,1,0:T(8,128)} fusion(f32[36,2,256]{2,1,0:T(2,128)S(1)} %collective-permute-done.7, f32[36,2,256]{2,1,0:T(2,128)S(1)} %collective-permute-done.6, f32[2,128,256]{2,1,0:T(8,128)S(1)} %collective-permute-done.5, f32[32,128,256]{2,1,0:T(8,128)S(1)} %get-tuple-element.31, f32[2,128,256]{2,1,0:T(8,128)S(1)} %collective-permute-done.4, ...), kind=kLoop, calls=%fused_computation.21 | loop fusion | flops 19768320 | bytes 9828180 | tf_op jit(solution)/shard_map/div | solution.py:104
  168.9 38.8 %fusion.28 = f32[32,128,256]{2,1,0:T(8,128)} fusion(f32[36,132,260]{2,1,0:T(8,128)} %fusion.5, s32[]{:T(128)S(6)} %select_n.1085, s32[]{:T(128)S(6)} %select_n.1086, s32[]{:T(128)S(6)} %select_n.1087, s32[]{:T(128)S(6)} %select_n.1082, s32[]{:T(128)S(6)} %select_n.1083, s32[]{:T(128)S(6)} %select_n.1084, s32[]{:T(128)S(6)} %select_n.1079, ...), kind=kLoop, calls=%fused_computation.65 | loop fusion | flops 14680064 | bytes 67108936 | tf_op jit(solution)/shard_map/add | solution.py:128
  208.9 3.1 collective-permute-start.8
  212.0 1.9 collective-permute-start.9
  215.3 5.4 %collective-permute-done.9 = f32[2,128,256]{2,1,0:T(8,128)S(1)} collective-permute-done((f32[2,128,256]{2,1,0:T(8,128)S(1)}, f32[2,128,256]{2,1,0:T(8,128)S(1)}, u32[]{:S(2)}, u32[]{:S(2)}) %collective-permute-start.9) | collective-permute-done | bytes 262176 | tf_op jit(solution)/shard_map/ppermute | solution.py:26
  221.8 7.3 %collective-permute-start.10 = (f32[36,2,256]{2,1,0:T(2,128)S(1)}, f32[36,2,256]{2,1,0:T(2,128)S(1)}, u32[]{:S(2)}, u32[]{:S(2)}) collective-permute-start(f32[36,2,256]{2,1,0:T(2,128)S(1)} %get-tuple-element.35), channel_id=1, source_target_pairs={{0,1},{1,2},{2,3},{3,4},{4,5},{5,6},{6,7},{8,9},{9,10},{10,11},{11... | collective-permute-start | bytes 221192 | tf_op jit(solution)/shard_map/ppermute | solution.py:24
  229.1 1.3 collective-permute-start.11
  230.4 1.3 and_convert_fusion.2
  231.7 2.5 collective-permute-done.11
  234.2 8.8 %fusion.3 = f32[36,132,260]{2,1,0:T(8,128)} fusion(f32[36,2,256]{2,1,0:T(2,128)S(1)} %collective-permute-done.11, f32[36,2,256]{2,1,0:T(2,128)S(1)} %collective-permute-done.10, f32[2,128,256]{2,1,0:T(8,128)S(1)} %collective-permute-done.9, f32[32,128,256]{2,1,0:T(8,128)S(1)} %copy-done.1, f32[2,128,256]{2,1,0:T(8,128)S(1)} %collective-permute-done.8, ...), kind=kLoop, calls=%fused_computation.15 | loop fusion | flops 19768320 | bytes 9828180 | tf_op jit(solution)/shard_map/div | solution.py:104
  243.0 38.7 %fusion.21 = f32[32,128,256]{2,1,0:T(8,128)} fusion(f32[36,132,260]{2,1,0:T(8,128)} %fusion.3, s32[]{:T(128)S(6)} %select_n.1085, s32[]{:T(128)S(6)} %select_n.1086, s32[]{:T(128)S(6)} %select_n.1087, s32[]{:T(128)S(6)} %select_n.1082, s32[]{:T(128)S(6)} %select_n.1083, s32[]{:T(128)S(6)} %select_n.1084, s32[]{:T(128)S(6)} %select_n.1079, ...), kind=kLoop, calls=%fused_computation.51 | loop fusion | flops 14680064 | bytes 67108936 | tf_op jit(solution)/shard_map/add | solution.py:128
  282.8 3.2 collective-permute-start.12
  286.0 2.1 collective-permute-start.13
  288.2 1.3 and_convert_fusion.1
  337.1 5.4 %collective-permute-start.14 = (f32[36,2,256]{2,1,0:T(2,128)S(1)}, f32[36,2,256]{2,1,0:T(2,128)S(1)}, u32[]{:S(2)}, u32[]{:S(2)}) collective-permute-start(f32[36,2,256]{2,1,0:T(2,128)S(1)} %get-tuple-element.33), channel_id=1, source_target_pairs={{0,1},{1,2},{2,3},{3,4},{4,5},{5,6},{6,7},{8,9},{9,10},{10,11},{11... | collective-permute-start | bytes 221192 | tf_op jit(solution)/shard_map/ppermute | solution.py:24
  342.5 1.3 collective-permute-start.15
  344.9 3.1 collective-permute-done.15
  348.1 8.8 %fusion.1 = f32[36,132,260]{2,1,0:T(8,128)} fusion(f32[36,2,256]{2,1,0:T(2,128)S(1)} %collective-permute-done.15, f32[36,2,256]{2,1,0:T(2,128)S(1)} %collective-permute-done.14, f32[2,128,256]{2,1,0:T(8,128)S(1)} %collective-permute-done.13, f32[32,128,256]{2,1,0:T(8,128)S(1)} %copy-done.2, f32[2,128,256]{2,1,0:T(8,128)S(1)} %collective-permute-done.12, ...), kind=kLoop, calls=%fused_computation.9 | loop fusion | flops 19768320 | bytes 9828180 | tf_op jit(solution)/shard_map/div | solution.py:104
  356.9 42.0 %fusion.13 = (f32[]{:T(128)}, f32[]{:T(128)}, f32[]{:T(128)}, f32[]{:T(128)}, f32[]{:T(128)}, /*index=5*/f32[]{:T(128)}, f32[]{:T(128)}, f32[]{:T(128)}, f32[]{:T(128)}, f32[]{:T(128)}, /*index=10*/f32[32,128,256]{2,1,0:T(8,128)}) fusion(f32[256]{0:T(256)S(1)} %and_convert_fusion, f32[32,128]{1,0:T(8,128)S(1)} %broadcast_multiply_fusion.13, ...), kind=kLoop, calls=%fused_computation.35 | loop fusion | flops 31457280 | bytes 79709296 | tf_op jit(solution)/shard_map/reduce_sum | solution.py:140
  398.9 75.1 %all-reduce.4 = (f32[]{:T(128)}, f32[]{:T(128)}, f32[]{:T(128)}, f32[]{:T(128)}, f32[]{:T(128)}, /*index=5*/f32[]{:T(128)}, f32[]{:T(128)}, f32[]{:T(128)}, f32[]{:T(128)}, f32[]{:T(128)}) all-reduce(f32[]{:T(128)} %get-tuple-element.18, f32[]{:T(128)} %get-tuple-element.16, ...), channel_id=1, replica_groups=mesh['gx'=16,'gy'=8] {'gx','gy'}, use_global_device_ids=true, to_apply=%region_11.12 | all-reduce | flops 10 | bytes 80 | tf_op jit(solution)/shard_map/psum | solution.py:141
  482.0 10.3 %multiply_add_fusion = f32[32,128,256]{2,1,0:T(8,128)} fusion(f32[32,128,256]{2,1,0:T(8,128)} %get-tuple-element.30, f32[32,128,256]{2,1,0:T(8,128)} %fusion.21, f32[32,128,256]{2,1,0:T(8,128)} %fusion.28, f32[32,128,256]{2,1,0:T(8,128)} %copy-done, f32[32,128,256]{2,1,0:T(8,128)} %param.5, f32[]{:T(128)S(6)} %add.881), kind=kLoop, calls=%fused_computation.97 | loop fusion | flops 11534336 | bytes 25165828 | tf_op jit(solution)/shard_map/add | solution.py:154
  (57 shorter events, 14.5 us)
Async XLA Ops:
  1.7 89.6 %collective-permute-start = (f32[2,128,256]{2,1,0:T(8,128)S(1)}, f32[2,128,256]{2,1,0:T(8,128)S(1)}, u32[]{:S(2)}, u32[]{:S(2)}) collective-permute-start(f32[2,128,256]{2,1,0:T(8,128)S(1)} %get-tuple-element.48), channel_id=1, source_target_pairs={{0,8},{8,16},{16,24},{24,32},{32,40},{40,48},{48,56},{56,64},{64,7... | collective-permute-start | bytes 786440 | tf_op jit(solution)/shard_map/ppermute | solution.py:24
  6.6 87.8 %collective-permute-start.1 = (f32[2,128,256]{2,1,0:T(8,128)S(1)}, f32[2,128,256]{2,1,0:T(8,128)S(1)}, u32[]{:S(2)}, u32[]{:S(2)}) collective-permute-start(f32[2,128,256]{2,1,0:T(8,128)S(1)} %get-tuple-element.47), channel_id=1, source_target_pairs={{8,0},{16,8},{24,16},{32,24},{40,32},{48,40},{56,48},{64,56},{72,6... | collective-permute-start | bytes 786440 | tf_op jit(solution)/shard_map/ppermute | solution.py:26
  91.3 16.0 %slice-start = ((s8[7520256]{0:T(1024)(128)(4,1)}), s8[4194304]{0:T(1024)(128)(4,1)S(1)}, s32[]{:S(2)}) async-start(s8[7520256]{0:T(1024)(128)(4,1)} %bitcast.182), calls=%async_computation | async-start | bytes 8388608
  94.5 5.6 %collective-permute-start.2 = (f32[36,2,256]{2,1,0:T(2,128)S(1)}, f32[36,2,256]{2,1,0:T(2,128)S(1)}, u32[]{:S(2)}, u32[]{:S(2)}) collective-permute-start(f32[36,2,256]{2,1,0:T(2,128)S(1)} %get-tuple-element.39), channel_id=1, source_target_pairs={{0,1},{1,2},{2,3},{3,4},{4,5},{5,6},{6,7},{8,9},{9,10},{10,11},{11... | collective-permute-start | bytes 221192 | tf_op jit(solution)/shard_map/ppermute | solution.py:24
  97.7 5.1 %collective-permute-start.3 = (f32[36,2,256]{2,1,0:T(2,128)S(1)}, f32[36,2,256]{2,1,0:T(2,128)S(1)}, u32[]{:S(2)}, u32[]{:S(2)}) collective-permute-start(f32[36,2,256]{2,1,0:T(2,128)S(1)} %get-tuple-element.40), channel_id=1, source_target_pairs={{1,0},{2,1},{3,2},{4,3},{5,4},{6,5},{7,6},{9,8},{10,9},{11,10},{12... | collective-permute-start | bytes 221192 | tf_op jit(solution)/shard_map/ppermute | solution.py:26
  100.1 7.2 %slice-start.1 = ((s8[7520256]{0:T(1024)(128)(4,1)}), s8[3325952]{0:T(1024)(128)(4,1)S(1)}, s32[]{:S(2)}) async-start(s8[7520256]{0:T(1024)(128)(4,1)} %bitcast.182), calls=%async_computation.1 | async-start | bytes 6651904
  138.7 30.2 %copy-start = (f32[32,128,256]{2,1,0:T(8,128)}, f32[32,128,256]{2,1,0:T(8,128)S(1)}, u32[]{:S(2)}) copy-start(f32[32,128,256]{2,1,0:T(8,128)S(1)} %get-tuple-element.31) | copy-start | bytes 12582916
  138.7 8.4 %collective-permute-start.4 = (f32[2,128,256]{2,1,0:T(8,128)S(1)}, f32[2,128,256]{2,1,0:T(8,128)S(1)}, u32[]{:S(2)}, u32[]{:S(2)}) collective-permute-start(f32[2,128,256]{2,1,0:T(8,128)S(1)} %get-tuple-element.45), channel_id=1, source_target_pairs={{0,8},{8,16},{16,24},{24,32},{32,40},{40,48},{48,56},{56,64},{64,7... | collective-permute-start | bytes 786440 | tf_op jit(solution)/shard_map/ppermute | solution.py:24
  143.8 7.7 %collective-permute-start.5 = (f32[2,128,256]{2,1,0:T(8,128)S(1)}, f32[2,128,256]{2,1,0:T(8,128)S(1)}, u32[]{:S(2)}, u32[]{:S(2)}) collective-permute-start(f32[2,128,256]{2,1,0:T(8,128)S(1)} %get-tuple-element.46), channel_id=1, source_target_pairs={{8,0},{16,8},{24,16},{32,24},{40,32},{48,40},{56,48},{64,56},{72,6... | collective-permute-start | bytes 786440 | tf_op jit(solution)/shard_map/ppermute | solution.py:26
  151.6 4.7 collective-permute-start.6
  154.8 5.3 %collective-permute-start.7 = (f32[36,2,256]{2,1,0:T(2,128)S(1)}, f32[36,2,256]{2,1,0:T(2,128)S(1)}, u32[]{:S(2)}, u32[]{:S(2)}) collective-permute-start(f32[36,2,256]{2,1,0:T(2,128)S(1)} %get-tuple-element.38), channel_id=1, source_target_pairs={{1,0},{2,1},{3,2},{4,3},{5,4},{6,5},{7,6},{9,8},{10,9},{11,10},{12... | collective-permute-start | bytes 221192 | tf_op jit(solution)/shard_map/ppermute | solution.py:26
  168.9 45.1 %copy-start.3 = (s32[2]{0:T(128)S(1)}, s32[2]{0:T(128)}, u32[]{:S(2)}) copy-start(s32[2]{0:T(128)} %param.9) | copy-start | bytes 28
  207.7 26.5 %copy-start.1 = (f32[32,128,256]{2,1,0:T(8,128)S(1)}, f32[32,128,256]{2,1,0:T(8,128)}, u32[]{:S(2)}) copy-start(f32[32,128,256]{2,1,0:T(8,128)} %fusion.28) | copy-start | bytes 12582916
  208.9 6.4 %collective-permute-start.8 = (f32[2,128,256]{2,1,0:T(8,128)S(1)}, f32[2,128,256]{2,1,0:T(8,128)S(1)}, u32[]{:S(2)}, u32[]{:S(2)}) collective-permute-start(f32[2,128,256]{2,1,0:T(8,128)S(1)} %get-tuple-element.43), channel_id=1, source_target_pairs={{0,8},{8,16},{16,24},{24,32},{32,40},{40,48},{48,56},{56,64},{64,7... | collective-permute-start | bytes 786440 | tf_op jit(solution)/shard_map/ppermute | solution.py:24
  212.0 8.7 %collective-permute-start.9 = (f32[2,128,256]{2,1,0:T(8,128)S(1)}, f32[2,128,256]{2,1,0:T(8,128)S(1)}, u32[]{:S(2)}, u32[]{:S(2)}) collective-permute-start(f32[2,128,256]{2,1,0:T(8,128)S(1)} %get-tuple-element.44), channel_id=1, source_target_pairs={{8,0},{16,8},{24,16},{32,24},{40,32},{48,40},{56,48},{64,56},{72,6... | collective-permute-start | bytes 786440 | tf_op jit(solution)/shard_map/ppermute | solution.py:26
  221.8 9.9 %collective-permute-start.10 = (f32[36,2,256]{2,1,0:T(2,128)S(1)}, f32[36,2,256]{2,1,0:T(2,128)S(1)}, u32[]{:S(2)}, u32[]{:S(2)}) collective-permute-start(f32[36,2,256]{2,1,0:T(2,128)S(1)} %get-tuple-element.35), channel_id=1, source_target_pairs={{0,1},{1,2},{2,3},{3,4},{4,5},{5,6},{6,7},{8,9},{9,10},{10,11},{11... | collective-permute-start | bytes 221192 | tf_op jit(solution)/shard_map/ppermute | solution.py:24
  229.1 5.1 %collective-permute-start.11 = (f32[36,2,256]{2,1,0:T(2,128)S(1)}, f32[36,2,256]{2,1,0:T(2,128)S(1)}, u32[]{:S(2)}, u32[]{:S(2)}) collective-permute-start(f32[36,2,256]{2,1,0:T(2,128)S(1)} %get-tuple-element.36), channel_id=1, source_target_pairs={{1,0},{2,1},{3,2},{4,3},{5,4},{6,5},{7,6},{9,8},{10,9},{11,10},{12... | collective-permute-start | bytes 221192 | tf_op jit(solution)/shard_map/ppermute | solution.py:26
  282.8 53.0 %collective-permute-start.12 = (f32[2,128,256]{2,1,0:T(8,128)S(1)}, f32[2,128,256]{2,1,0:T(8,128)S(1)}, u32[]{:S(2)}, u32[]{:S(2)}) collective-permute-start(f32[2,128,256]{2,1,0:T(8,128)S(1)} %get-tuple-element.41), channel_id=1, source_target_pairs={{0,8},{8,16},{16,24},{24,32},{32,40},{40,48},{48,56},{56,64},{64,7... | collective-permute-start | bytes 786440 | tf_op jit(solution)/shard_map/ppermute | solution.py:24
  286.0 49.9 %collective-permute-start.13 = (f32[2,128,256]{2,1,0:T(8,128)S(1)}, f32[2,128,256]{2,1,0:T(8,128)S(1)}, u32[]{:S(2)}, u32[]{:S(2)}) collective-permute-start(f32[2,128,256]{2,1,0:T(8,128)S(1)} %get-tuple-element.42), channel_id=1, source_target_pairs={{8,0},{16,8},{24,16},{32,24},{40,32},{48,40},{56,48},{64,56},{72,6... | collective-permute-start | bytes 786440 | tf_op jit(solution)/shard_map/ppermute | solution.py:26
  335.8 12.3 %copy-start.2 = (f32[32,128,256]{2,1,0:T(8,128)S(1)}, f32[32,128,256]{2,1,0:T(8,128)}, u32[]{:S(2)}) copy-start(f32[32,128,256]{2,1,0:T(8,128)} %fusion.21) | copy-start | bytes 12582916
  337.1 7.8 %collective-permute-start.14 = (f32[36,2,256]{2,1,0:T(2,128)S(1)}, f32[36,2,256]{2,1,0:T(2,128)S(1)}, u32[]{:S(2)}, u32[]{:S(2)}) collective-permute-start(f32[36,2,256]{2,1,0:T(2,128)S(1)} %get-tuple-element.33), channel_id=1, source_target_pairs={{0,1},{1,2},{2,3},{3,4},{4,5},{5,6},{6,7},{8,9},{9,10},{10,11},{11... | collective-permute-start | bytes 221192 | tf_op jit(solution)/shard_map/ppermute | solution.py:24
  342.5 5.5 %collective-permute-start.15 = (f32[36,2,256]{2,1,0:T(2,128)S(1)}, f32[36,2,256]{2,1,0:T(2,128)S(1)}, u32[]{:S(2)}, u32[]{:S(2)}) collective-permute-start(f32[36,2,256]{2,1,0:T(2,128)S(1)} %get-tuple-element.34), channel_id=1, source_target_pairs={{1,0},{2,1},{3,2},{4,3},{5,4},{6,5},{7,6},{9,8},{10,9},{11,10},{12... | collective-permute-start | bytes 221192 | tf_op jit(solution)/shard_map/ppermute | solution.py:26
where the time goes:
time: 495 us; the launch traced here: 492 us
  other arithmetic  228 us (46%)
  between operations  103 us (21%)
  blocking collectives  75.1 us (15%)
  starting transfers between devices  48.6 us (10%)
  waiting for transfers between devices  24 us (5%)
  local copies, waits for them, and re-layouts  13.1 us (3%)
    add x3, other arithmetic, advance(): advanced = advanced + arrival  109 us
    psum x1, blocking collectives, record(): local_sums = lax.psum((local_sums[0], local_sums[1]), ('gx', 'gy'))  75.1 us
    reduce_sum x1, other arithmetic, record(): local_sums = (jnp.sum(current), jnp.sum(current * interior_box))  42 us
    ppermute x8, starting transfers between devices, extended_2(): lax.ppermute(tail, axis, [(i, (i + 1) % count) for i in range(ends)])  35.4 us
    div x4, other arithmetic, advance(): scaled = padded * free / uniform_rate  31 us
    ppermute x8, waiting for transfers between devices, extended_2(): lax.ppermute(head, axis, [((i + 1) % count, i) for i in range(ends)])  21.9 us
    mul x14, other arithmetic, outer_three(): along_first[:, None, None] * along_second[None, :, None]  21.4 us
    ppermute x8, starting transfers between devices, extended_2(): lax.ppermute(head, axis, [((i + 1) % count, i) for i in range(ends)])  13.3 us
  transfers between devices with their start and end apart: 16, of which 8 were waited for; matrix products, arithmetic and copies ran while one was open for 9% of the time, Pallas kernels for 0%

commit v1 on v0

v1 whole, which is shorter than its diff:
```python
import functools
import math

import jax
import jax.numpy as jnp
from jax import lax
from jax.experimental import pallas as pl
from jax.experimental.pallas import tpu as pltpu
from jax.sharding import PartitionSpec as P

STEPS = 4
mean_jumps = 8.0
headroom = 1.05
series_length = 40
TABLE = [
    math.exp(-mean_jumps) * mean_jumps**k / math.factorial(k) for k in range(series_length)
]
MESH = pl.DeviceIdType.MESH
LANES = 128
PAD = 8
MOVES = [(-1, 0), (1, 0), (0, -1), (0, 1), (-1, -1), (-1, 1), (1, -1), (1, 1)]
BACK = [1, 0, 3, 2, 7, 6, 5, 4]


def quadratic(order, extent):
    zero = jnp.float32(0.0)
    return (
        jnp.where(order == 0, jnp.float32(1.0), zero),
        jnp.where(order == 1, jnp.float32(1.0 / extent), zero),
        jnp.where(order == 2, jnp.float32(1.0 / (extent * extent)), zero),
    )


def evaluate(coefficients, m):
    c0, c1, c2 = coefficients
    return c0 + c1 * m + c2 * (m * (m - 1.0))


def kernel(
    nx, ny, bx, by, reactions,
    density, rates, changes, box, truncation,
    occupancy, summary,
    p, s, d, shifted_b, plain_b, free_table, box_table,
    recv_x, recv_y, recv_c, send_y, send_c, red_y, red_x,
    load_sem, store_sem, send_sem, recv_sem, ysend_sem, yrecv_sem, xsend_sem, xrecv_sem,
):
    me_x, me_y = lax.axis_index("gx"), lax.axis_index("gy")
    anchor_x, anchor_y = me_x * bx, me_y * by
    extents = (nx * bx, ny * by, 2 * LANES)
    yp = by + 2 * PAD
    plane = (bx + 4) * yp

    def present(move):
        px, py = me_x + move[0], me_y + move[1]
        return (px >= 0) & (px < nx) & (py >= 0) & (py < ny)

    exists = [present(move) for move in MOVES]

    loads = [
        pltpu.make_async_copy(
            density.at[:, pl.ds(h * LANES, LANES)], p.at[0, h], load_sem.at[h]
        )
        for h in range(2)
    ]
    for load in loads:
        load.start()

    barrier = pltpu.get_barrier_semaphore()

    def greet(px, py):
        pl.semaphore_signal(barrier, inc=1, device_id=(px, py), device_id_type=MESH)

    @pl.loop(1, nx)
    def _(step):
        greet(lax.rem(me_x + step, nx), me_y)

    @pl.loop(1, ny)
    def _(step):
        greet(me_x, lax.rem(me_y + step, ny))

    corners = jnp.int32(0)
    for way in range(4, 8):
        corners = corners + exists[way].astype(jnp.int32)

        @pl.when(exists[way])
        def _():
            greet(me_x + MOVES[way][0], me_y + MOVES[way][1])

    order = [[jnp.maximum(-changes[r, a], 0) for a in range(3)] for r in range(reactions)]
    phi = [[quadratic(order[r][a], float(extents[a])) for a in range(3)] for r in range(reactions)]
    corner = None
    for r in range(reactions):
        term = rates[r]
        for a in range(3):
            term = term * evaluate(phi[r][a], jnp.float32(extents[a] - 1))
        corner = term if corner is None else corner + term
    inverse_rate = 1.0 / jnp.full((8, LANES), headroom * corner, jnp.float32)
    inverse_rate = inverse_rate[0:1]
    tails = []
    for which in range(2):
        tail = jnp.float32(0.0)
        for k in range(STEPS + 1, series_length):
            tail = tail + jnp.where(k <= truncation[which], jnp.float32(TABLE[k]), jnp.float32(0.0))
        tails.append(tail)
    offsets = [
        (changes[r, 2] + 2) * (2 * plane) + (2 - changes[r, 0]) * yp + (PAD - changes[r, 1])
        for r in range(reactions)
    ]

    def within(count, a):
        return (count >= box[0, a]) & (count < box[1, a])

    def along_x(x_local, move):
        out = []
        for r in range(reactions):
            count = anchor_x + x_local
            if move:
                count = count - changes[r, 0]
            out.append(rates[r] * evaluate(phi[r][0], count.astype(jnp.float32)))
        return out

    def lanes(rows):
        return lax.broadcasted_iota(jnp.int32, (rows, LANES), 1)

    z_count = [lanes(1) + h * LANES for h in range(2)]
    z_float = [z.astype(jnp.float32) for z in z_count]
    z_box = [within(z, 2).astype(jnp.float32) for z in z_count]
    z_one = [z * (1.0 / extents[2]) for z in z_float]
    z_two = [z * (z - 1.0) * (1.0 / extents[2] ** 2) for z in z_float]

    rows = lax.broadcasted_iota(jnp.int32, (by, LANES), 0) + anchor_y
    for r in range(reactions):
        shifted_b[r] = evaluate(phi[r][1], (rows - changes[r, 1]).astype(jnp.float32))
        plain_b[r] = evaluate(phi[r][1], rows.astype(jnp.float32))
    y_box = within(rows, 1).astype(jnp.float32)
    for h in range(2):
        inside = y_box * z_box[h]
        free_table[0, h] = jnp.broadcast_to(inverse_rate, (by, LANES))
        free_table[1, h] = inverse_rate * (1.0 - inside)
        box_table[0, h] = jnp.zeros((by, LANES), jnp.float32)
        box_table[1, h] = inside

    for side, way in ((0, 0), (1, 1)):

        @pl.when(jnp.logical_not(exists[way]))
        def _():
            @pl.loop(0, 10)
            def _(part):
                start = part * plane + (side * (bx + 2)) * yp
                s[pl.ds(pl.multiple_of(start, 8), 2 * yp), :] = jnp.zeros((2 * yp, LANES), jnp.float32)

    for side, way in ((0, 2), (1, 3)):

        @pl.when(jnp.logical_not(exists[way]))
        def _():
            @pl.loop(0, 10 * (bx + 4))
            def _(part):
                start = part * yp + side * (by + PAD)
                s[pl.ds(pl.multiple_of(start, 8), 8), :] = jnp.zeros((8, LANES), jnp.float32)

    for k in range(STEPS):
        for c in range(4):
            send_c[k, c] = jnp.zeros((2, 8, LANES), jnp.float32)

    def halo_copy(k, way):
        px, py = me_x + MOVES[way][0], me_y + MOVES[way][1]
        land = BACK[way]
        if way < 2:
            start = 0 if way == 0 else (bx - 2) * by
            source = p.at[k, :, pl.ds(start, 2 * by), :]
            target = recv_x.at[k, land]
        elif way < 4:
            source = send_y.at[k, way - 2]
            target = recv_y.at[k, land - 2]
        else:
            source = send_c.at[k, way - 4]
            target = recv_c.at[k, land - 4]
        return pltpu.make_async_remote_copy(
            src_ref=source,
            dst_ref=target,
            send_sem=send_sem.at[k, way],
            recv_sem=recv_sem.at[k, land],
            device_id=(px, py),
            device_id_type=MESH,
        )

    def arrived(k, way):
        return pltpu.make_async_remote_copy(
            src_ref=(p.at[k, :, pl.ds(0, 2 * by), :] if way < 2 else send_y.at[k, way - 2] if way < 4 else send_c.at[k, way - 4]),
            dst_ref=(recv_x.at[k, way] if way < 2 else recv_y.at[k, way - 2] if way < 4 else recv_c.at[k, way - 4]),
            send_sem=send_sem.at[k, way],
            recv_sem=recv_sem.at[k, way],
            device_id=(me_x + MOVES[way][0], me_y + MOVES[way][1]),
            device_id_type=MESH,
        )

    def send_faces(k, ways):
        for way in ways:

            @pl.when(exists[way])
            def _():
                halo_copy(k, way).start()

    def pack(k):
        for side in range(2):
            for j in range(2):
                y = j if side == 0 else by - 2 + j
                for h in range(2):
                    send_y[k, side, pl.ds((j * 2 + h) * bx, bx), :] = p[k, h, pl.ds(y, bx, stride=by), :]
        for c in range(4):
            x0 = 0 if MOVES[4 + c][0] < 0 else bx - 2
            y0 = 0 if MOVES[4 + c][1] < 0 else by - 2
            for h in range(2):
                for x in range(2):
                    send_c[k, c, h, pl.ds(2 * x, 2), :] = p[k, h, pl.ds((x0 + x) * by + y0, 2), :]

    def shifts(c0, c1, f0, f1):
        lane = lanes(c0.shape[0])
        zero = jnp.zeros_like(c0)
        a0, a1 = c0 * f0, c1 * f1
        out = []
        for v in range(-2, 3):
            if v == 0:
                out.append((a0, a1))
                continue
            if v > 0:
                t0, t1 = pltpu.roll(a0, v, 1), pltpu.roll(a1, v, 1)
                out.append((jnp.where(lane < v, zero, t0), jnp.where(lane < v, t0, t1)))
            else:
                factor = z_one if v == -1 else z_two
                t0 = pltpu.roll(a0 * factor[0], LANES + v, 1)
                t1 = pltpu.roll(a1 * factor[1], LANES + v, 1)
                edge = lane >= LANES + v
                out.append((jnp.where(edge, t1, t0), jnp.where(edge, zero, t1)))
        return out

    chunk = min(64, by)

    def scale_plane(x_local, load):
        taken = within(anchor_x + x_local, 0).astype(jnp.int32)
        for y0 in range(0, by, chunk):
            c0, c1 = load(0, y0), load(1, y0)
            f0 = free_table[taken, 0, pl.ds(y0, chunk), :]
            f1 = free_table[taken, 1, pl.ds(y0, chunk), :]
            row = pl.multiple_of((x_local + 2) * yp + (PAD + y0), 8)
            for v, pair in enumerate(shifts(c0, c1, f0, f1)):
                for h in range(2):
                    s[pl.ds((v * 2 + h) * plane + row, chunk), :] = pair[h]

    def scale_own(k):
        @pl.loop(0, bx)
        def _(x):
            base = pl.multiple_of(x * by, 8)
            scale_plane(x, lambda h, y0: p[k, h, pl.ds(base + y0, chunk), :])

    def scale_halo(k):
        for way in range(2):

            @pl.when(exists[way])
            def _():
                arrived(k, way).wait_recv()
                for i in range(2):
                    x = i - 2 if way == 0 else bx + i
                    scale_plane(
                        jnp.int32(x),
                        lambda h, y0: recv_x[k, way, h, pl.ds(i * by + y0, chunk), :],
                    )

        x_row = lax.broadcasted_iota(jnp.int32, (bx, LANES), 0) + anchor_x
        x_box = within(x_row, 0).astype(jnp.float32)
        for way in range(2, 4):

            @pl.when(exists[way])
            def _():
                arrived(k, way).wait_recv()
                for j in range(2):
                    y = j - 2 if way == 2 else by + j
                    inside = x_box * within(anchor_y + y, 1).astype(jnp.float32)
                    c0 = recv_y[k, way - 2, pl.ds((j * 2) * bx, bx), :]
                    c1 = recv_y[k, way - 2, pl.ds((j * 2 + 1) * bx, bx), :]
                    f0 = inverse_rate * (1.0 - inside * z_box[0])
                    f1 = inverse_rate * (1.0 - inside * z_box[1])
                    for v, pair in enumerate(shifts(c0, c1, f0, f1)):
                        for h in range(2):
                            s[pl.ds((v * 2 + h) * plane + 2 * yp + PAD + y, bx, stride=yp), :] = pair[h]

        small = lax.broadcasted_iota(jnp.int32, (8, LANES), 0)
        for way in range(4, 8):

            @pl.when(exists[way])
            def _():
                arrived(k, way).wait_recv()
                x0 = -2 if MOVES[way][0] < 0 else bx
                y0 = -2 if MOVES[way][1] < 0 else by
                inside = (
                    within(anchor_x + x0 + (small >> 1), 0) & within(anchor_y + y0 + (small & 1), 1)
                ).astype(jnp.float32)
                c0 = recv_c[k, way - 4, 0]
                c1 = recv_c[k, way - 4, 1]
                f0 = inverse_rate * (1.0 - inside * z_box[0])
                f1 = inverse_rate * (1.0 - inside * z_box[1])
                for v, pair in enumerate(shifts(c0, c1, f0, f1)):
                    for h in range(2):
                        for x in range(2):
                            row = (v * 2 + h) * plane + (x0 + x + 2) * yp + PAD + y0
                            s[pl.ds(row, 2), :] = pair[h][2 * x : 2 * x + 2]

    def advance(k, x, factors, y0, n):
        base = pl.multiple_of(x * by + y0, 8)
        total = [p[k, h, pl.ds(base, n), :] * d[h, pl.ds(base, n), :] for h in range(2)]
        for r in range(reactions):
            along = factors[r] * shifted_b[r, pl.ds(y0, n), :]
            for h in range(2):
                row = offsets[r] + (x * yp + (h * plane + y0))
                total[h] = total[h] + along * s[pl.ds(row, n), :]
        return base, total

    def advance_to(k, x, spans):
        factors = along_x(x, True)
        for y0, n in spans:
            base, total = advance(k, x, factors, y0, n)
            for h in range(2):
                p[k + 1, h, pl.ds(base, n), :] = total[h]

    half = by // 2
    whole = [(0, half), (half, half)]
    inner = (by - 16) // 2
    middle = [(8, inner), (8 + inner, inner)]

    def self_term():
        z_factor = [
            [
                jnp.where(order[r][2] == 0, jnp.ones_like(z_one[h]), jnp.where(order[r][2] == 1, z_one[h], z_two[h]))
                for h in range(2)
            ]
            for r in range(reactions)
        ]

        @pl.loop(0, bx)
        def _(x):
            factors = along_x(x, False)
            taken = within(anchor_x + x, 0).astype(jnp.int32)
            for y0, n in whole:
                total = [None, None]
                for r in range(reactions):
                    along = factors[r] * plain_b[r, pl.ds(y0, n), :]
                    for h in range(2):
                        term = along * z_factor[r][h]
                        total[h] = term if total[h] is None else total[h] + term
                for h in range(2):
                    base = pl.multiple_of(x * by + y0, 8)
                    d[h, pl.ds(base, n), :] = 1.0 - total[h] * free_table[taken, h, pl.ds(y0, n), :]

    for load in loads:
        load.wait()
    pl.semaphore_wait(barrier, nx - 1 + ny - 1 + corners)
    send_faces(0, (0, 1))
    pack(0)
    send_faces(0, range(2, 8))
    scale_own(0)
    self_term()

    @pl.loop(0, STEPS - 1)
    def _(k):
        scale_halo(k)
        for x0 in (0, bx - 2):

            @pl.loop(x0, x0 + 2)
            def _(x):
                advance_to(k, x, whole)

        send_faces(k + 1, (0, 1))

        @pl.loop(2, bx - 2)
        def _(x):
            advance_to(k, x, [(0, 8), (by - 8, 8)])

        pack(k + 1)
        send_faces(k + 1, range(2, 8))

        @pl.loop(2, bx - 2)
        def _(x):
            advance_to(k, x, middle)

        scale_own(k + 1)

    last = STEPS - 1
    scale_halo(last)
    weights = [jnp.float32(TABLE[k]) for k in range(STEPS + 1)]
    weight_density = weights[STEPS] + tails[0]
    weight_total = weights[STEPS] + tails[1]

    def finish(x, carry):
        mass, hit = carry
        factors = along_x(x, True)
        taken = within(anchor_x + x, 0).astype(jnp.int32)
        for y0, n in whole:
            base, total = advance(last, x, factors, y0, n)
            for h in range(2):
                earlier = weights[0] * p[0, h, pl.ds(base, n), :]
                for k in range(1, STEPS):
                    earlier = earlier + weights[k] * p[k, h, pl.ds(base, n), :]
                d[h, pl.ds(base, n), :] = earlier + weight_density * total[h]
                counted = earlier + weight_total * total[h]
                struck = counted * box_table[taken, h, pl.ds(y0, n), :]
                mass = mass + jnp.sum(counted.reshape(n // 8, 8, LANES), axis=0)
                hit = hit + jnp.sum(struck.reshape(n // 8, 8, LANES), axis=0)
        return mass, hit

    zero = jnp.zeros((8, LANES), jnp.float32)
    mass, hit = lax.fori_loop(0, bx, finish, (zero, zero))

    stores = [
        pltpu.make_async_copy(
            d.at[h], occupancy.at[:, pl.ds(h * LANES, LANES)], store_sem.at[h]
        )
        for h in range(2)
    ]
    for store in stores:
        store.start()

    row8 = lax.broadcasted_iota(jnp.int32, (8, LANES), 0)
    red_y[me_y] = jnp.where(
        row8 == 0,
        jnp.sum(mass, axis=0, keepdims=True),
        jnp.where(row8 == 1, jnp.sum(hit, axis=0, keepdims=True), 0.0),
    )

    def share(ref, size, mine, send, recv, device):
        def copy(step, slot):
            return pltpu.make_async_remote_copy(
                src_ref=ref.at[mine],
                dst_ref=ref.at[slot],
                send_sem=send.at[step],
                recv_sem=recv.at[step],
                device_id=device(lax.rem(mine + step, size)),
                device_id_type=MESH,
            )

        @pl.loop(1, size)
        def _(step):
            copy(step, mine).start()

        @pl.loop(1, size)
        def _(step):
            copy(step, lax.rem(mine + size - step, size)).wait_recv()

        @pl.loop(1, size)
        def _(step):
            copy(step, mine).wait_send()

        total = ref[0]
        for slot in range(1, size):
            total = total + ref[slot]
        return total

    red_x[me_x] = share(red_y, ny, me_y, ysend_sem, yrecv_sem, lambda other: (me_x, other))
    total = share(red_x, nx, me_x, xsend_sem, xrecv_sem, lambda other: (other, me_y))
    cells = float(extents[0] * extents[1] * extents[2])
    summary[0] = jnp.sum(total[1:2]) * jnp.float32(1.0 / cells)
    summary[1] = jnp.sum(total[0:1]) * jnp.float32(1.0 / cells)

    for k in range(STEPS):
        for way in range(8):

            @pl.when(exists[way])
            def _():
                halo_copy(k, way).wait_send()

    for store in stores:
        store.wait()


def body(nx, ny, density, reaction_rates, state_changes, target_box, truncation):
    bx, by, nz = density.shape
    reactions = state_changes.shape[0]
    yp = by + 2 * PAD
    f32 = jnp.float32
    vmem = lambda *shape: pltpu.VMEM(shape, f32)
    dma = pltpu.SemaphoreType.DMA
    occupancy, summary = pl.pallas_call(
        functools.partial(kernel, nx, ny, bx, by, reactions),
        out_shape=(
            jax.ShapeDtypeStruct((bx * by, nz), f32),
            jax.ShapeDtypeStruct((2,), f32),
        ),
        in_specs=[pl.BlockSpec(memory_space=pl.ANY)]
        + [pl.BlockSpec(memory_space=pltpu.SMEM)] * 4,
        out_specs=(
            pl.BlockSpec(memory_space=pl.ANY),
            pl.BlockSpec(memory_space=pltpu.SMEM),
        ),
        scratch_shapes=[
            vmem(STEPS, 2, bx * by, LANES),
            vmem(10 * (bx + 4) * yp, LANES),
            vmem(2, bx * by, LANES),
            vmem(reactions, by, LANES),
            vmem(reactions, by, LANES),
            vmem(2, 2, by, LANES),
            vmem(2, 2, by, LANES),
            vmem(STEPS, 2, 2, 2 * by, LANES),
            vmem(STEPS, 2, 4 * bx, LANES),
            vmem(STEPS, 4, 2, 8, LANES),
            vmem(STEPS, 2, 4 * bx, LANES),
            vmem(STEPS, 4, 2, 8, LANES),
            vmem(ny, 8, LANES),
            vmem(nx, 8, LANES),
            dma((2,)),
            dma((2,)),
            dma((STEPS, 8)),
            dma((STEPS, 8)),
            dma((ny,)),
            dma((ny,)),
            dma((nx,)),
            dma((nx,)),
        ],
        compiler_params=pltpu.CompilerParams(
            collective_id=0, has_side_effects=True, vmem_limit_bytes=60 * 1024 * 1024
        ),
    )(density.reshape(bx * by, nz), reaction_rates, state_changes, target_box, truncation)
    return occupancy.reshape(bx, by, nz), summary


def solution(mesh):
    placed = (P("gx", "gy", None), P(), P(), P(), P())
    return jax.shard_map(
        functools.partial(body, mesh.shape["gx"], mesh.shape["gy"]),
        mesh=mesh,
        in_specs=placed,
        out_specs=(P("gx", "gy", None), P()),
        check_vma=False,
    )
```

time: 495 us -> 85.1 us (0.17)
  other arithmetic: 228 us -> 0 us
  between operations: 103 us -> 0.65 us
  Pallas kernels: 0 us -> 77.7 us
  blocking collectives: 75.1 us -> 0 us
  starting transfers between devices: 48.6 us -> 0 us
  waiting for transfers between devices: 24 us -> 0 us
  local copies, waits for them, and re-layouts: 13.1 us -> 6.53 us
    add x4 -> x0, other arithmetic: 119 us -> none  [the longest x3 109 us: advance(): advanced = advanced + arrival]
    pallas_call x0 -> x1, Pallas kernels: none -> 77.7 us  [body(): pl.pallas_call(functools.partial(kernel, nx, ny, bx, by, reactions), out_...]
    psum x1 -> x0, blocking collectives: 75.1 us -> none  [record(): local_sums = lax.psum((local_sums[0], local_sums[1]), ('gx', 'gy'))]
    ppermute x16 -> x0, starting transfers between devices: 48.6 us -> none  [the longest x8 35.4 us: extended_2(): lax.ppermute(tail, axis, [(i, (i + 1) % count) for i in range(ends)])]
    reduce_sum x1 -> x0, other arithmetic: 42 us -> none  [record(): local_sums = (jnp.sum(current), jnp.sum(current * interior_box))]
    div x4 -> x0, other arithmetic: 31 us -> none  [advance(): scaled = padded * free / uniform_rate]
    mul x17 -> x0, other arithmetic: 25.1 us -> none  [the longest x14 21.4 us: outer_three(): along_first[:, None, None] * along_second[None, :, None]]
    ppermute x16 -> x0, waiting for transfers between devices: 24 us -> none  [the longest x8 21.9 us: extended_2(): lax.ppermute(head, axis, [((i + 1) % count, i) for i in range(ends)])]
  transfers between devices with their start and end apart: 16 -> 0, of which waited for: 8 -> 0; matrix products, arithmetic and copies ran while one was open for 9% -> 0% of each run, Pallas kernels for 0% -> 0%
where the time goes in v1:
time: 85.1 us; the launch traced here: 84.9 us
  Pallas kernels  77.7 us (91%)
  local copies, waits for them, and re-layouts  6.53 us (8%)
    pallas_call x1, Pallas kernels, body(): pl.pallas_call(functools.partial(kernel, nx, ny, bx, by, reactions), out_...  77.7 us
    unnamed x5, local copies, waits for them, and re-layouts  6.53 us

profile of v1, /device:TPU:1, one launch (start us, length us, event | category | flops | bytes accessed | tf_op | source)
XLA Modules:
  0.0 84.9 jit_solution(4800710388598628429)
XLA Ops:
  0.6 1.4 %copy.7.changes = s32[6,3]{1,0:T(8,128)} copy(s32[6,3]{0,1:T(4,128)} %param.7) | data formatting | bytes 144 | tf_op args[2]
  2.0 77.7 %shard_map.68 = (f32[4096,256]{1,0:T(8,128)}, f32[2]{0:T(128)}) custom-call(f32[4096,256]{1,0:T(8,128)} %bitcast.2, f32[6]{0:T(128)} %rates.1, s32[6,3]{1,0:T(8,128)} %copy.7.changes, s32[2,3]{1,0:T(2,128)} %box.1, s32[2]{0:T(128)} %truncation.1), custom_call_target="tpu_custom_call" | custom-call | tf_op jit(solution)/shard_map/pallas_call | solution.py:481
  79.7 0.0 copy-start
  79.7 4.7 %copy.10 = f32[32,128,256]{2,1,0:T(8,128)} copy(f32[32,128,256]{2,1,0:T(8,128)} %bitcast.3) | data formatting | bytes 8388608
  84.4 0.0 copy-done
  84.4 0.5 copy.11
Async XLA Ops:
  79.7 4.7 %copy-start = (f32[2]{0:T(128)S(1)}, f32[2]{0:T(128)}, u32[]{:S(2)}) copy-start(f32[2]{0:T(128)} %get-tuple-element.9) | copy-start | bytes 28

commit v2 on v1

--- a/solution.py
+++ b/solution.py
@@ -17,6 +17,8 @@
 ]
 MESH = pl.DeviceIdType.MESH
 LANES = 128
+GROUP = 8
+MOVED = (1, 2)
 PAD = 8
 MOVES = [(-1, 0), (1, 0), (0, -1), (0, 1), (-1, -1), (-1, 1), (1, -1), (1, 1)]
 BACK = [1, 0, 3, 2, 7, 6, 5, 4]
@@ -40,7 +42,7 @@
     nx, ny, bx, by, reactions,
     density, rates, changes, box, truncation,
     occupancy, summary,
-    p, s, d, shifted_b, plain_b, free_table, box_table,
+    p, s, d, parts, movers, shifted_b, plain_b, free_table, box_table,
     recv_x, recv_y, recv_c, send_y, send_c, red_y, red_x,
     load_sem, store_sem, send_sem, recv_sem, ysend_sem, yrecv_sem, xsend_sem, xrecv_sem,
 ):
@@ -86,7 +88,7 @@
         def _():
             greet(me_x + MOVES[way][0], me_y + MOVES[way][1])
 
-    order = [[jnp.maximum(-changes[r, a], 0) for a in range(3)] for r in range(reactions)]
+    order = [[jnp.maximum(-changes[a, r], 0) for a in range(3)] for r in range(reactions)]
     phi = [[quadratic(order[r][a], float(extents[a])) for a in range(3)] for r in range(reactions)]
     corner = None
     for r in range(reactions):
@@ -103,7 +105,7 @@
             tail = tail + jnp.where(k <= truncation[which], jnp.float32(TABLE[k]), jnp.float32(0.0))
         tails.append(tail)
     offsets = [
-        (changes[r, 2] + 2) * (2 * plane) + (2 - changes[r, 0]) * yp + (PAD - changes[r, 1])
+        (changes[2, r] + 2) * (2 * plane) + (2 - changes[0, r]) * yp + (PAD - changes[1, r])
         for r in range(reactions)
     ]
 
@@ -115,7 +117,7 @@
         for r in range(reactions):
             count = anchor_x + x_local
             if move:
-                count = count - changes[r, 0]
+                count = count - changes[0, r]
             out.append(rates[r] * evaluate(phi[r][0], count.astype(jnp.float32)))
         return out
 
@@ -128,9 +130,16 @@
     z_one = [z * (1.0 / extents[2]) for z in z_float]
     z_two = [z * (z - 1.0) * (1.0 / extents[2] ** 2) for z in z_float]
 
+    z_two_after = [(z + 2.0) * (z + 1.0) * (1.0 / extents[2] ** 2) for z in z_float]
+    source = lax.broadcasted_iota(jnp.int32, (4 * LANES, 2 * LANES), 0) & (2 * LANES - 1)
+    target = lax.broadcasted_iota(jnp.int32, (4 * LANES, 2 * LANES), 1)
+    for m, v in enumerate(MOVED):
+        weight = source.astype(jnp.float32) * (1.0 / extents[2]) if v == -1 else jnp.float32(1.0)
+        movers[m] = jnp.where(target - source == v, weight, 0.0).astype(jnp.bfloat16)
+
     rows = lax.broadcasted_iota(jnp.int32, (by, LANES), 0) + anchor_y
     for r in range(reactions):
-        shifted_b[r] = evaluate(phi[r][1], (rows - changes[r, 1]).astype(jnp.float32))
+        shifted_b[r] = evaluate(phi[r][1], (rows - changes[1, r]).astype(jnp.float32))
         plain_b[r] = evaluate(phi[r][1], rows.astype(jnp.float32))
     y_box = within(rows, 1).astype(jnp.float32)
     for h in range(2):
@@ -214,7 +223,7 @@
                 for x in range(2):
                     send_c[k, c, h, pl.ds(2 * x, 2), :] = p[k, h, pl.ds((x0 + x) * by + y0, 2), :]
 
-    def shifts(c0, c1, f0, f1):
+    def shifts(c0, c1, f0, f1, skip=()):
         lane = lanes(c0.shape[0])
         zero = jnp.zeros_like(c0)
         a0, a1 = c0 * f0, c1 * f1
@@ -222,6 +231,9 @@
         for v in range(-2, 3):
             if v == 0:
                 out.append((a0, a1))
+                continue
+            if v in skip:
+                out.append(None)
                 continue
             if v > 0:
                 t0, t1 = pltpu.roll(a0, v, 1), pltpu.roll(a1, v, 1)
@@ -236,22 +248,47 @@
 
     chunk = min(64, by)
 
-    def scale_plane(x_local, load):
+    def scale_plane(x_local, load, slot=None):
         taken = within(anchor_x + x_local, 0).astype(jnp.int32)
         for y0 in range(0, by, chunk):
             c0, c1 = load(0, y0), load(1, y0)
             f0 = free_table[taken, 0, pl.ds(y0, chunk), :]
             f1 = free_table[taken, 1, pl.ds(y0, chunk), :]
             row = pl.multiple_of((x_local + 2) * yp + (PAD + y0), 8)
-            for v, pair in enumerate(shifts(c0, c1, f0, f1)):
+            for v, pair in enumerate(shifts(c0, c1, f0, f1, MOVED if slot is not None else ())):
+                if pair is None:
+                    continue
                 for h in range(2):
                     s[pl.ds((v * 2 + h) * plane + row, chunk), :] = pair[h]
+                if v == 2 and slot is not None:
+                    for h in range(2):
+                        high = pair[h].astype(jnp.bfloat16)
+                        low = (pair[h] - high.astype(jnp.float32)).astype(jnp.bfloat16)
+                        here = pl.ds(slot * by + y0, chunk)
+                        parts[here, pl.ds(h * LANES, LANES)] = high
+                        parts[here, pl.ds((2 + h) * LANES, LANES)] = low
+
+    def move_planes(x_first, planes):
+        for m, v in enumerate(MOVED):
+            moved = jnp.dot(
+                parts[pl.ds(0, planes * by), :], movers[m], preferred_element_type=jnp.float32
+            )
+            for h in range(2):
+                for i in range(planes):
+                    value = moved[i * by : (i + 1) * by, h * LANES : (h + 1) * LANES]
+                    if v == -2:
+                        value = value * z_two_after[h]
+                    row = pl.multiple_of((x_first + i + 2) * yp + PAD, 8)
+                    s[pl.ds(((v + 2) * 2 + h) * plane + row, by), :] = value
 
     def scale_own(k):
-        @pl.loop(0, bx)
-        def _(x):
-            base = pl.multiple_of(x * by, 8)
-            scale_plane(x, lambda h, y0: p[k, h, pl.ds(base + y0, chunk), :])
+        @pl.loop(0, bx // GROUP)
+        def _(group):
+            first = group * GROUP
+            for i in range(GROUP):
+                base = pl.multiple_of((first + i) * by, 8)
+                scale_plane(first + i, lambda h, y0: p[k, h, pl.ds(base + y0, chunk), :], i)
+            move_planes(first, GROUP)
 
     def scale_halo(k):
         for way in range(2):
@@ -264,7 +301,9 @@
                     scale_plane(
                         jnp.int32(x),
                         lambda h, y0: recv_x[k, way, h, pl.ds(i * by + y0, chunk), :],
+                        i,
                     )
+                move_planes(-2 if way == 0 else bx, 2)
 
         x_row = lax.broadcasted_iota(jnp.int32, (bx, LANES), 0) + anchor_x
         x_box = within(x_row, 0).astype(jnp.float32)
@@ -371,14 +410,14 @@
 
         send_faces(k + 1, (0, 1))
 
-        @pl.loop(2, bx - 2)
+        @pl.loop(2, bx - 2, unroll=4)
         def _(x):
             advance_to(k, x, [(0, 8), (by - 8, 8)])
 
         pack(k + 1)
         send_faces(k + 1, range(2, 8))
 
-        @pl.loop(2, bx - 2)
+        @pl.loop(2, bx - 2, unroll=2)
         def _(x):
             advance_to(k, x, middle)
 
@@ -494,6 +533,8 @@
             vmem(STEPS, 2, bx * by, LANES),
             vmem(10 * (bx + 4) * yp, LANES),
             vmem(2, bx * by, LANES),
+            pltpu.VMEM((GROUP * by, 4 * LANES), jnp.bfloat16),
+            pltpu.VMEM((len(MOVED), 4 * LANES, 2 * LANES), jnp.bfloat16),
             vmem(reactions, by, LANES),
             vmem(reactions, by, LANES),
             vmem(2, 2, by, LANES),
@@ -517,7 +558,7 @@
         compiler_params=pltpu.CompilerParams(
             collective_id=0, has_side_effects=True, vmem_limit_bytes=60 * 1024 * 1024
         ),
-    )(density.reshape(bx * by, nz), reaction_rates, state_changes, target_box, truncation)
+    )(density.reshape(bx * by, nz), reaction_rates, state_changes.T, target_box, truncation)
     return occupancy.reshape(bx, by, nz), summary
 
 

time: 85.1 us -> 69.1 us (0.81)
  Pallas kernels: 77.7 us -> 63.2 us
  local copies, waits for them, and re-layouts: 6.53 us -> 5.17 us
    pallas_call x1, Pallas kernels: 77.7 us -> 63.2 us  [body(): pl.pallas_call(functools.partial(kernel, nx, ny, bx, by, reactions), out_...]
    unnamed x5 -> x4, local copies, waits for them, and re-layouts: 6.53 us -> 5.17 us
where the time goes in v2:
time: 69.1 us; the launch traced here: 69 us
  Pallas kernels  63.2 us (91%)
  local copies, waits for them, and re-layouts  5.17 us (7%)
    pallas_call x1, Pallas kernels, body(): pl.pallas_call(functools.partial(kernel, nx, ny, bx, by, reactions), out_...  63.2 us
    unnamed x4, local copies, waits for them, and re-layouts  5.17 us

profile of v2, /device:TPU:1, one launch (start us, length us, event | category | flops | bytes accessed | tf_op | source)
XLA Modules:
  0.0 69.0 jit_solution(12173729805225863541)
XLA Ops:
  0.6 63.2 %shard_map.68 = (f32[4096,256]{1,0:T(8,128)}, f32[2]{0:T(128)}) custom-call(f32[4096,256]{1,0:T(8,128)} %bitcast.3, f32[6]{0:T(128)} %rates.1, s32[3,6]{1,0:T(4,128)} %bitcast.5, s32[2,3]{1,0:T(2,128)} %box.1, s32[2]{0:T(128)} %truncation.1), custom_call_target="tpu_custom_call" | custom-call | tf_op jit(solution)/shard_map/pallas_call | solution.py:520
  63.8 0.0 copy-start
  63.8 4.7 %copy.9 = f32[32,128,256]{2,1,0:T(8,128)} copy(f32[32,128,256]{2,1,0:T(8,128)} %bitcast.4) | data formatting | bytes 8388608
  68.5 0.0 copy-done
  68.5 0.5 copy.10
Async XLA Ops:
  63.8 4.7 %copy-start = (f32[2]{0:T(128)S(1)}, f32[2]{0:T(128)}, u32[]{:S(2)}) copy-start(f32[2]{0:T(128)} %get-tuple-element.9) | copy-start | bytes 28

commit v3 on v2

--- a/solution.py
+++ b/solution.py
@@ -44,7 +44,7 @@
     occupancy, summary,
     p, s, d, parts, movers, shifted_b, plain_b, free_table, box_table,
     recv_x, recv_y, recv_c, send_y, send_c, red_y, red_x,
-    load_sem, store_sem, send_sem, recv_sem, ysend_sem, yrecv_sem, xsend_sem, xrecv_sem,
+    load_sem, send_sem, recv_sem, ysend_sem, yrecv_sem, xsend_sem, xrecv_sem,
 ):
     me_x, me_y = lax.axis_index("gx"), lax.axis_index("gy")
     anchor_x, anchor_y = me_x * bx, me_y * by
@@ -87,85 +87,6 @@
         @pl.when(exists[way])
         def _():
             greet(me_x + MOVES[way][0], me_y + MOVES[way][1])
-
-    order = [[jnp.maximum(-changes[a, r], 0) for a in range(3)] for r in range(reactions)]
-    phi = [[quadratic(order[r][a], float(extents[a])) for a in range(3)] for r in range(reactions)]
-    corner = None
-    for r in range(reactions):
-        term = rates[r]
-        for a in range(3):
-            term = term * evaluate(phi[r][a], jnp.float32(extents[a] - 1))
-        corner = term if corner is None else corner + term
-    inverse_rate = 1.0 / jnp.full((8, LANES), headroom * corner, jnp.float32)
-    inverse_rate = inverse_rate[0:1]
-    tails = []
-    for which in range(2):
-        tail = jnp.float32(0.0)
-        for k in range(STEPS + 1, series_length):
-            tail = tail + jnp.where(k <= truncation[which], jnp.float32(TABLE[k]), jnp.float32(0.0))
-        tails.append(tail)
-    offsets = [
-        (changes[2, r] + 2) * (2 * plane) + (2 - changes[0, r]) * yp + (PAD - changes[1, r])
-        for r in range(reactions)
-    ]
-
-    def within(count, a):
-        return (count >= box[0, a]) & (count < box[1, a])
-
-    def along_x(x_local, move):
-        out = []
-        for r in range(reactions):
-            count = anchor_x + x_local
-            if move:
-                count = count - changes[0, r]
-            out.append(rates[r] * evaluate(phi[r][0], count.astype(jnp.float32)))
-        return out
-
-    def lanes(rows):
-        return lax.broadcasted_iota(jnp.int32, (rows, LANES), 1)
-
-    z_count = [lanes(1) + h * LANES for h in range(2)]
-    z_float = [z.astype(jnp.float32) for z in z_count]
-    z_box = [within(z, 2).astype(jnp.float32) for z in z_count]
-    z_one = [z * (1.0 / extents[2]) for z in z_float]
-    z_two = [z * (z - 1.0) * (1.0 / extents[2] ** 2) for z in z_float]
-
-    z_two_after = [(z + 2.0) * (z + 1.0) * (1.0 / extents[2] ** 2) for z in z_float]
-    source = lax.broadcasted_iota(jnp.int32, (4 * LANES, 2 * LANES), 0) & (2 * LANES - 1)
-    target = lax.broadcasted_iota(jnp.int32, (4 * LANES, 2 * LANES), 1)
-    for m, v in enumerate(MOVED):
-        weight = source.astype(jnp.float32) * (1.0 / extents[2]) if v == -1 else jnp.float32(1.0)
-        movers[m] = jnp.where(target - source == v, weight, 0.0).astype(jnp.bfloat16)
-
-    rows = lax.broadcasted_iota(jnp.int32, (by, LANES), 0) + anchor_y
-    for r in range(reactions):
-        shifted_b[r] = evaluate(phi[r][1], (rows - changes[1, r]).astype(jnp.float32))
-        plain_b[r] = evaluate(phi[r][1], rows.astype(jnp.float32))
-    y_box = within(rows, 1).astype(jnp.float32)
-    for h in range(2):
-        inside = y_box * z_box[h]
-        free_table[0, h] = jnp.broadcast_to(inverse_rate, (by, LANES))
-        free_table[1, h] = inverse_rate * (1.0 - inside)
-        box_table[0, h] = jnp.zeros((by, LANES), jnp.float32)
-        box_table[1, h] = inside
-
-    for side, way in ((0, 0), (1, 1)):
-
-        @pl.when(jnp.logical_not(exists[way]))
-        def _():
-            @pl.loop(0, 10)
-            def _(part):
-                start = part * plane + (side * (bx + 2)) * yp
-                s[pl.ds(pl.multiple_of(start, 8), 2 * yp), :] = jnp.zeros((2 * yp, LANES), jnp.float32)
-
-    for side, way in ((0, 2), (1, 3)):
-
-        @pl.when(jnp.logical_not(exists[way]))
-        def _():
-            @pl.loop(0, 10 * (bx + 4))
-            def _(part):
-                start = part * yp + side * (by + PAD)
-                s[pl.ds(pl.multiple_of(start, 8), 8), :] = jnp.zeros((8, LANES), jnp.float32)
 
     for k in range(STEPS):
         for c in range(4):
@@ -222,6 +143,86 @@
             for h in range(2):
                 for x in range(2):
                     send_c[k, c, h, pl.ds(2 * x, 2), :] = p[k, h, pl.ds((x0 + x) * by + y0, 2), :]
+
+    for load in loads:
+        load.wait()
+    pl.semaphore_wait(barrier, nx - 1 + ny - 1 + corners)
+    send_faces(0, (0, 1))
+    pack(0)
+    send_faces(0, range(2, 8))
+
+    order = [[jnp.maximum(-changes[a, r], 0) for a in range(3)] for r in range(reactions)]
+    phi = [[quadratic(order[r][a], float(extents[a])) for a in range(3)] for r in range(reactions)]
+    corner = None
+    for r in range(reactions):
+        term = rates[r]
+        for a in range(3):
+            term = term * evaluate(phi[r][a], jnp.float32(extents[a] - 1))
+        corner = term if corner is None else corner + term
+    inverse_rate = 1.0 / jnp.full((8, LANES), headroom * corner, jnp.float32)
+    inverse_rate = inverse_rate[0:1]
+    tails = []
+    for which in range(2):
+        tail = jnp.float32(0.0)
+        for k in range(STEPS + 1, series_length):
+            tail = tail + jnp.where(k <= truncation[which], jnp.float32(TABLE[k]), jnp.float32(0.0))
+        tails.append(tail)
+    offsets = [
+        (changes[2, r] + 2) * (2 * plane) + (2 - changes[0, r]) * yp + (PAD - changes[1, r])
+        for r in range(reactions)
+    ]
+
+    def within(count, a):
+        return (count >= box[0, a]) & (count < box[1, a])
+
+    def along_x(x_local, move):
+        out = []
+        for r in range(reactions):
+            count = anchor_x + x_local
+            if move:
+                count = count - changes[0, r]
+            out.append(rates[r] * evaluate(phi[r][0], count.astype(jnp.float32)))
+        return out
+
+    def lanes(rows):
+        return lax.broadcasted_iota(jnp.int32, (rows, LANES), 1)
+
+    z_count = [lanes(1) + h * LANES for h in range(2)]
+    z_float = [z.astype(jnp.float32) for z in z_count]
+    z_box = [within(z, 2).astype(jnp.float32) for z in z_count]
+    z_one = [z * (1.0 / extents[2]) for z in z_float]
+    z_two = [z * (z - 1.0) * (1.0 / extents[2] ** 2) for z in z_float]
+
+    z_two_after = [(z + 2.0) * (z + 1.0) * (1.0 / extents[2] ** 2) for z in z_float]
+    source = lax.broadcasted_iota(jnp.int32, (4 * LANES, 2 * LANES), 0) & (2 * LANES - 1)
+    target = lax.broadcasted_iota(jnp.int32, (4 * LANES, 2 * LANES), 1)
+    for m, v in enumerate(MOVED):
+        weight = source.astype(jnp.float32) * (1.0 / extents[2]) if v == -1 else jnp.float32(1.0)
+        movers[m] = jnp.where(target - source == v, weight, 0.0).astype(jnp.bfloat16)
+
+    rows = lax.broadcasted_iota(jnp.int32, (by, LANES), 0) + anchor_y
+    for r in range(reactions):
+        shifted_b[r] = evaluate(phi[r][1], (rows - changes[1, r]).astype(jnp.float32))
+        plain_b[r] = evaluate(phi[r][1], rows.astype(jnp.float32))
+    y_box = within(rows, 1).astype(jnp.float32)
+    for h in range(2):
+        inside = y_box * z_box[h]
+        free_table[0, h] = jnp.broadcast_to(inverse_rate, (by, LANES))
+        free_table[1, h] = inverse_rate * (1.0 - inside)
+        box_table[0, h] = jnp.zeros((by, LANES), jnp.float32)
+        box_table[1, h] = inside
+
+    for way in range(8):
+
+        @pl.when(jnp.logical_not(exists[way]))
+        def _():
+            for k in range(STEPS):
+                if way < 2:
+                    recv_x[k, way] = jnp.zeros((2, 2 * by, LANES), jnp.float32)
+                elif way < 4:
+                    recv_y[k, way - 2] = jnp.zeros((4 * bx, LANES), jnp.float32)
+                else:
+                    recv_c[k, way - 4] = jnp.zeros((2, 8, LANES), jnp.float32)
 
     def shifts(c0, c1, f0, f1, skip=()):
         lane = lanes(c0.shape[0])
@@ -268,17 +269,17 @@
                         parts[here, pl.ds(h * LANES, LANES)] = high
                         parts[here, pl.ds((2 + h) * LANES, LANES)] = low
 
-    def move_planes(x_first, planes):
+    def move_planes(xs):
         for m, v in enumerate(MOVED):
             moved = jnp.dot(
-                parts[pl.ds(0, planes * by), :], movers[m], preferred_element_type=jnp.float32
+                parts[pl.ds(0, len(xs) * by), :], movers[m], preferred_element_type=jnp.float32
             )
             for h in range(2):
-                for i in range(planes):
+                for i, x in enumerate(xs):
                     value = moved[i * by : (i + 1) * by, h * LANES : (h + 1) * LANES]
                     if v == -2:
                         value = value * z_two_after[h]
-                    row = pl.multiple_of((x_first + i + 2) * yp + PAD, 8)
+                    row = pl.multiple_of((x + 2) * yp + PAD, 8)
                     s[pl.ds(((v + 2) * 2 + h) * plane + row, by), :] = value
 
     def scale_own(k):
@@ -288,61 +289,56 @@
             for i in range(GROUP):
                 base = pl.multiple_of((first + i) * by, 8)
                 scale_plane(first + i, lambda h, y0: p[k, h, pl.ds(base + y0, chunk), :], i)
-            move_planes(first, GROUP)
-
-    def scale_halo(k):
-        for way in range(2):
+            move_planes([first + i for i in range(GROUP)])
+
+    def await_halo(k, ways):
+        for way in ways:
 
             @pl.when(exists[way])
             def _():
                 arrived(k, way).wait_recv()
-                for i in range(2):
-                    x = i - 2 if way == 0 else bx + i
-                    scale_plane(
-                        jnp.int32(x),
-                        lambda h, y0: recv_x[k, way, h, pl.ds(i * by + y0, chunk), :],
-                        i,
-                    )
-                move_planes(-2 if way == 0 else bx, 2)
-
+
+    def scale_halo(k):
+        await_halo(k, range(2, 8))
         x_row = lax.broadcasted_iota(jnp.int32, (bx, LANES), 0) + anchor_x
         x_box = within(x_row, 0).astype(jnp.float32)
         for way in range(2, 4):
-
-            @pl.when(exists[way])
-            def _():
-                arrived(k, way).wait_recv()
-                for j in range(2):
-                    y = j - 2 if way == 2 else by + j
-                    inside = x_box * within(anchor_y + y, 1).astype(jnp.float32)
-                    c0 = recv_y[k, way - 2, pl.ds((j * 2) * bx, bx), :]
-                    c1 = recv_y[k, way - 2, pl.ds((j * 2 + 1) * bx, bx), :]
-                    f0 = inverse_rate * (1.0 - inside * z_box[0])
-                    f1 = inverse_rate * (1.0 - inside * z_box[1])
-                    for v, pair in enumerate(shifts(c0, c1, f0, f1)):
-                        for h in range(2):
-                            s[pl.ds((v * 2 + h) * plane + 2 * yp + PAD + y, bx, stride=yp), :] = pair[h]
-
-        small = lax.broadcasted_iota(jnp.int32, (8, LANES), 0)
-        for way in range(4, 8):
-
-            @pl.when(exists[way])
-            def _():
-                arrived(k, way).wait_recv()
-                x0 = -2 if MOVES[way][0] < 0 else bx
-                y0 = -2 if MOVES[way][1] < 0 else by
-                inside = (
-                    within(anchor_x + x0 + (small >> 1), 0) & within(anchor_y + y0 + (small & 1), 1)
-                ).astype(jnp.float32)
-                c0 = recv_c[k, way - 4, 0]
-                c1 = recv_c[k, way - 4, 1]
+            for j in range(2):
+                y = j - 2 if way == 2 else by + j
+                inside = x_box * within(anchor_y + y, 1).astype(jnp.float32)
+                c0 = recv_y[k, way - 2, pl.ds((j * 2) * bx, bx), :]
+                c1 = recv_y[k, way - 2, pl.ds((j * 2 + 1) * bx, bx), :]
                 f0 = inverse_rate * (1.0 - inside * z_box[0])
                 f1 = inverse_rate * (1.0 - inside * z_box[1])
                 for v, pair in enumerate(shifts(c0, c1, f0, f1)):
                     for h in range(2):
-                        for x in range(2):
-                            row = (v * 2 + h) * plane + (x0 + x + 2) * yp + PAD + y0
-                            s[pl.ds(row, 2), :] = pair[h][2 * x : 2 * x + 2]
+                        s[pl.ds((v * 2 + h) * plane + 2 * yp + PAD + y, bx, stride=yp), :] = pair[h]
+        small = lax.broadcasted_iota(jnp.int32, (8, LANES), 0)
+        for way in range(4, 8):
+            x0 = -2 if MOVES[way][0] < 0 else bx
+            y0 = -2 if MOVES[way][1] < 0 else by
+            inside = (
+                within(anchor_x + x0 + (small >> 1), 0) & within(anchor_y + y0 + (small & 1), 1)
+            ).astype(jnp.float32)
+            c0 = recv_c[k, way - 4, 0]
+            c1 = recv_c[k, way - 4, 1]
+            f0 = inverse_rate * (1.0 - inside * z_box[0])
+            f1 = inverse_rate * (1.0 - inside * z_box[1])
+            for v, pair in enumerate(shifts(c0, c1, f0, f1)):
+                for h in range(2):
+                    for x in range(2):
+                        row = (v * 2 + h) * plane + (x0 + x + 2) * yp + PAD + y0
+                        s[pl.ds(row, 2), :] = pair[h][2 * x : 2 * x + 2]
+        await_halo(k, range(2))
+        places = [(way, i) for way in range(2) for i in range(2)]
+        xs = [i - 2 if way == 0 else bx + i for way, i in places]
+        for slot, (way, i) in enumerate(places):
+            scale_plane(
+                jnp.int32(xs[slot]),
+                lambda h, y0: recv_x[k, way, h, pl.ds(i * by + y0, chunk), :],
+                slot,
+            )
+        move_planes(xs)
 
     def advance(k, x, factors, y0, n):
         base = pl.multiple_of(x * by + y0, 8)
@@ -365,6 +361,11 @@
     whole = [(0, half), (half, half)]
     inner = (by - 16) // 2
     middle = [(8, inner), (8 + inner, inner)]
+
+    def advance_middle(k):
+        @pl.loop(2, bx - 2, unroll=2)
+        def _(x):
+            advance_to(k, x, middle)
 
     def self_term():
         z_factor = [
@@ -390,14 +391,9 @@
                     base = pl.multiple_of(x * by + y0, 8)
                     d[h, pl.ds(base, n), :] = 1.0 - total[h] * free_table[taken, h, pl.ds(y0, n), :]
 
-    for load in loads:
-        load.wait()
-    pl.semaphore_wait(barrier, nx - 1 + ny - 1 + corners)
-    send_faces(0, (0, 1))
-    pack(0)
-    send_faces(0, range(2, 8))
     scale_own(0)
     self_term()
+    advance_middle(0)
 
     @pl.loop(0, STEPS - 1)
     def _(k):
@@ -417,29 +413,28 @@
         pack(k + 1)
         send_faces(k + 1, range(2, 8))
 
-        @pl.loop(2, bx - 2, unroll=2)
-        def _(x):
-            advance_to(k, x, middle)
-
         scale_own(k + 1)
 
+        @pl.when(k + 1 < STEPS - 1)
+        def _():
+            advance_middle(k + 1)
+
     last = STEPS - 1
-    scale_halo(last)
     weights = [jnp.float32(TABLE[k]) for k in range(STEPS + 1)]
     weight_density = weights[STEPS] + tails[0]
     weight_total = weights[STEPS] + tails[1]
 
-    def finish(x, carry):
+    def finish(spans, x, carry):
         mass, hit = carry
         factors = along_x(x, True)
         taken = within(anchor_x + x, 0).astype(jnp.int32)
-        for y0, n in whole:
+        for y0, n in spans:
             base, total = advance(last, x, factors, y0, n)
             for h in range(2):
                 earlier = weights[0] * p[0, h, pl.ds(base, n), :]
                 for k in range(1, STEPS):
                     earlier = earlier + weights[k] * p[k, h, pl.ds(base, n), :]
-                d[h, pl.ds(base, n), :] = earlier + weight_density * total[h]
+                occupancy[pl.ds(base, n), pl.ds(h * LANES, LANES)] = earlier + weight_density * total[h]
                 counted = earlier + weight_total * total[h]
                 struck = counted * box_table[taken, h, pl.ds(y0, n), :]
                 mass = mass + jnp.sum(counted.reshape(n // 8, 8, LANES), axis=0)
@@ -447,16 +442,12 @@
         return mass, hit
 
     zero = jnp.zeros((8, LANES), jnp.float32)
-    mass, hit = lax.fori_loop(0, bx, finish, (zero, zero))
-
-    stores = [
-        pltpu.make_async_copy(
-            d.at[h], occupancy.at[:, pl.ds(h * LANES, LANES)], store_sem.at[h]
-        )
-        for h in range(2)
-    ]
-    for store in stores:
-        store.start()
+    sums = lax.fori_loop(2, bx - 2, functools.partial(finish, middle), (zero, zero))
+    scale_halo(last)
+    for x0 in (0, bx - 2):
+        sums = lax.fori_loop(x0, x0 + 2, functools.partial(finish, whole), sums)
+    edges = functools.partial(finish, [(0, 8), (by - 8, 8)])
+    mass, hit = lax.fori_loop(2, bx - 2, edges, sums, unroll=4)
 
     row8 = lax.broadcasted_iota(jnp.int32, (8, LANES), 0)
     red_y[me_y] = jnp.where(
@@ -465,49 +456,45 @@
         jnp.where(row8 == 1, jnp.sum(hit, axis=0, keepdims=True), 0.0),
     )
 
-    def share(ref, size, mine, send, recv, device):
-        def copy(step, slot):
-            return pltpu.make_async_remote_copy(
-                src_ref=ref.at[mine],
-                dst_ref=ref.at[slot],
-                send_sem=send.at[step],
-                recv_sem=recv.at[step],
-                device_id=device(lax.rem(mine + step, size)),
-                device_id_type=MESH,
-            )
-
-        @pl.loop(1, size)
-        def _(step):
-            copy(step, mine).start()
-
-        @pl.loop(1, size)
-        def _(step):
-            copy(step, lax.rem(mine + size - step, size)).wait_recv()
-
-        @pl.loop(1, size)
-        def _(step):
-            copy(step, mine).wait_send()
-
+    def share_copy(ref, size, mine, send, recv, device, step, slot):
+        return pltpu.make_async_remote_copy(
+            src_ref=ref.at[mine],
+            dst_ref=ref.at[slot],
+            send_sem=send.at[step],
+            recv_sem=recv.at[step],
+            device_id=device(lax.rem(mine + step, size)),
+            device_id_type=MESH,
+        )
+
+    def share(*group):
+        ref, size, mine = group[:3]
+        for step in range(1, size):
+            share_copy(*group, step, mine).start()
+        for step in range(1, size):
+            share_copy(*group, step, lax.rem(mine + size - step, size)).wait_recv()
         total = ref[0]
         for slot in range(1, size):
             total = total + ref[slot]
         return total
 
-    red_x[me_x] = share(red_y, ny, me_y, ysend_sem, yrecv_sem, lambda other: (me_x, other))
-    total = share(red_x, nx, me_x, xsend_sem, xrecv_sem, lambda other: (other, me_y))
+    along_gy = (red_y, ny, me_y, ysend_sem, yrecv_sem, lambda other: (me_x, other))
+    along_gx = (red_x, nx, me_x, xsend_sem, xrecv_sem, lambda other: (other, me_y))
+    red_x[me_x] = share(*along_gy)
+    total = share(*along_gx)
     cells = float(extents[0] * extents[1] * extents[2])
     summary[0] = jnp.sum(total[1:2]) * jnp.float32(1.0 / cells)
     summary[1] = jnp.sum(total[0:1]) * jnp.float32(1.0 / cells)
 
+    for step in range(1, ny):
+        share_copy(*along_gy, step, me_y).wait_send()
+    for step in range(1, nx):
+        share_copy(*along_gx, step, me_x).wait_send()
     for k in range(STEPS):
         for way in range(8):
 
             @pl.when(exists[way])
             def _():
                 halo_copy(k, way).wait_send()
-
-    for store in stores:
-        store.wait()
 
 
 def body(nx, ny, density, reaction_rates, state_changes, target_box, truncation):
@@ -520,13 +507,13 @@
     occupancy, summary = pl.pallas_call(
         functools.partial(kernel, nx, ny, bx, by, reactions),
         out_shape=(
-            jax.ShapeDtypeStruct((bx * by, nz), f32),
+            pltpu.VMEM((bx * by, nz), f32),
             jax.ShapeDtypeStruct((2,), f32),
         ),
         in_specs=[pl.BlockSpec(memory_space=pl.ANY)]
         + [pl.BlockSpec(memory_space=pltpu.SMEM)] * 4,
         out_specs=(
-            pl.BlockSpec(memory_space=pl.ANY),
+            pl.BlockSpec(memory_space=pltpu.VMEM),
             pl.BlockSpec(memory_space=pltpu.SMEM),
         ),
         scratch_shapes=[
@@ -547,7 +534,6 @@
             vmem(ny, 8, LANES),
             vmem(nx, 8, LANES),
             dma((2,)),
-            dma((2,)),
             dma((STEPS, 8)),
             dma((STEPS, 8)),
             dma((ny,)),
@@ -556,7 +542,7 @@
             dma((nx,)),
         ],
         compiler_params=pltpu.CompilerParams(
-            collective_id=0, has_side_effects=True, vmem_limit_bytes=60 * 1024 * 1024
+            collective_id=0, has_side_effects=True, vmem_limit_bytes=54 * 1024 * 1024
         ),
     )(density.reshape(bx * by, nz), reaction_rates, state_changes.T, target_box, truncation)
     return occupancy.reshape(bx, by, nz), summary

time: 69.1 us -> 64.3 us (0.931)
  local copies, waits for them, and re-layouts: 5.17 us -> 2.53 us
  Pallas kernels: 63.2 us -> 61 us
    unnamed x4, local copies, waits for them, and re-layouts: 5.17 us -> 2.53 us
    pallas_call x1, Pallas kernels: 63.2 us -> 61 us  [body(): pl.pallas_call(functools.partial(kernel, nx, ny, bx, by, reactions), out_...]
where the time goes in v3:
time: 64.3 us; the launch traced here: 64.2 us
  Pallas kernels  61 us (95%)
  local copies, waits for them, and re-layouts  2.53 us (4%)
  between operations  0.65 us (1%)
    pallas_call x1, Pallas kernels, body(): pl.pallas_call(functools.partial(kernel, nx, ny, bx, by, reactions), out_...  61 us
    unnamed x4, local copies, waits for them, and re-layouts  2.53 us

profile of v3, /device:TPU:1, one launch (start us, length us, event | category | flops | bytes accessed | tf_op | source)
XLA Modules:
  0.0 64.2 jit_solution(16778327854207163760)
XLA Ops:
  0.6 61.0 %shard_map.68 = (f32[4096,256]{1,0:T(8,128)S(1)}, f32[2]{0:T(128)}) custom-call(f32[4096,256]{1,0:T(8,128)} %bitcast.4, f32[6]{0:T(128)} %rates.1, s32[3,6]{1,0:T(4,128)} %bitcast.5, s32[2,3]{1,0:T(2,128)} %box.1, s32[2]{0:T(128)} %truncation.1), custom_call_target="tpu_custom_call" | custom-call | tf_op jit(solution)/shard_map/pallas_call | solution.py:507
  61.7 0.0 copy-start
  61.7 2.0 %copy.9 = f32[32,128,256]{2,1,0:T(8,128)} copy(f32[32,128,256]{2,1,0:T(8,128)S(1)} %bitcast.3) | data formatting | bytes 8388608
  63.7 0.0 copy-done
  63.7 0.5 copy.10
Async XLA Ops:
  61.7 2.0 %copy-start = (f32[2]{0:T(128)S(1)}, f32[2]{0:T(128)}, u32[]{:S(2)}) copy-start(f32[2]{0:T(128)} %get-tuple-element.11) | copy-start | bytes 28

commit v4 on v3

--- a/solution.py
+++ b/solution.py
@@ -43,8 +43,8 @@
     density, rates, changes, box, truncation,
     occupancy, summary,
     p, s, d, parts, movers, shifted_b, plain_b, free_table, box_table,
-    recv_x, recv_y, recv_c, send_y, send_c, red_y, red_x,
-    load_sem, send_sem, recv_sem, ysend_sem, yrecv_sem, xsend_sem, xrecv_sem,
+    recv_x, recv_y, recv_c, send_y, send_c, red_near, red_far,
+    load_sem, send_sem, recv_sem, nsend_sem, nrecv_sem, fsend_sem, frecv_sem,
 ):
     me_x, me_y = lax.axis_index("gx"), lax.axis_index("gy")
     anchor_x, anchor_y = me_x * bx, me_y * by
@@ -72,21 +72,41 @@
     def greet(px, py):
         pl.semaphore_signal(barrier, inc=1, device_id=(px, py), device_id_type=MESH)
 
-    @pl.loop(1, nx)
-    def _(step):
-        greet(lax.rem(me_x + step, nx), me_y)
-
-    @pl.loop(1, ny)
-    def _(step):
-        greet(me_x, lax.rem(me_y + step, ny))
-
-    corners = jnp.int32(0)
-    for way in range(4, 8):
-        corners = corners + exists[way].astype(jnp.int32)
-
-        @pl.when(exists[way])
+    inner_x, outer_y = 4, 2
+    outer_x, inner_y = nx // inner_x, ny // outer_y
+    near_size, far_size = inner_x * outer_y, outer_x * inner_y
+    near_me = (me_x % inner_x) * outer_y + me_y // inner_y
+    far_me = (me_x // inner_x) * inner_y + me_y % inner_y
+
+    def near_device(other):
+        return (
+            (me_x // inner_x) * inner_x + other // outer_y,
+            (other % outer_y) * inner_y + me_y % inner_y,
+        )
+
+    def far_device(other):
+        return (
+            (other // inner_y) * inner_x + me_x % inner_x,
+            (me_y // inner_y) * inner_y + other % inner_y,
+        )
+
+    for size, mine, device in ((near_size, near_me, near_device), (far_size, far_me, far_device)):
+
+        @pl.loop(1, size)
+        def _(step):
+            greet(*device((mine + step) % size))
+
+    others = jnp.int32(0)
+    for way in range(8):
+        px, py = me_x + MOVES[way][0], me_y + MOVES[way][1]
+        is_near = (px // inner_x == me_x // inner_x) & (py % inner_y == me_y % inner_y)
+        is_far = (px % inner_x == me_x % inner_x) & (py // inner_y == me_y // inner_y)
+        alone = exists[way] & jnp.logical_not(is_near | is_far)
+        others = others + alone.astype(jnp.int32)
+
+        @pl.when(alone)
         def _():
-            greet(me_x + MOVES[way][0], me_y + MOVES[way][1])
+            greet(px, py)
 
     for k in range(STEPS):
         for c in range(4):
@@ -146,7 +166,7 @@
 
     for load in loads:
         load.wait()
-    pl.semaphore_wait(barrier, nx - 1 + ny - 1 + corners)
+    pl.semaphore_wait(barrier, near_size - 1 + far_size - 1 + others)
     send_faces(0, (0, 1))
     pack(0)
     send_faces(0, range(2, 8))
@@ -442,7 +462,7 @@
         return mass, hit
 
     zero = jnp.zeros((8, LANES), jnp.float32)
-    sums = lax.fori_loop(2, bx - 2, functools.partial(finish, middle), (zero, zero))
+    sums = lax.fori_loop(2, bx - 2, functools.partial(finish, middle), (zero, zero), unroll=2)
     scale_halo(last)
     for x0 in (0, bx - 2):
         sums = lax.fori_loop(x0, x0 + 2, functools.partial(finish, whole), sums)
@@ -450,7 +470,7 @@
     mass, hit = lax.fori_loop(2, bx - 2, edges, sums, unroll=4)
 
     row8 = lax.broadcasted_iota(jnp.int32, (8, LANES), 0)
-    red_y[me_y] = jnp.where(
+    red_near[near_me] = jnp.where(
         row8 == 0,
         jnp.sum(mass, axis=0, keepdims=True),
         jnp.where(row8 == 1, jnp.sum(hit, axis=0, keepdims=True), 0.0),
@@ -477,18 +497,18 @@
             total = total + ref[slot]
         return total
 
-    along_gy = (red_y, ny, me_y, ysend_sem, yrecv_sem, lambda other: (me_x, other))
-    along_gx = (red_x, nx, me_x, xsend_sem, xrecv_sem, lambda other: (other, me_y))
-    red_x[me_x] = share(*along_gy)
-    total = share(*along_gx)
+    near = (red_near, near_size, near_me, nsend_sem, nrecv_sem, near_device)
+    far = (red_far, far_size, far_me, fsend_sem, frecv_sem, far_device)
+    red_far[far_me] = share(*near)
+    total = share(*far)
     cells = float(extents[0] * extents[1] * extents[2])
     summary[0] = jnp.sum(total[1:2]) * jnp.float32(1.0 / cells)
     summary[1] = jnp.sum(total[0:1]) * jnp.float32(1.0 / cells)
 
-    for step in range(1, ny):
-        share_copy(*along_gy, step, me_y).wait_send()
-    for step in range(1, nx):
-        share_copy(*along_gx, step, me_x).wait_send()
+    for step in range(1, near_size):
+        share_copy(*near, step, near_me).wait_send()
+    for step in range(1, far_size):
+        share_copy(*far, step, far_me).wait_send()
     for k in range(STEPS):
         for way in range(8):
 

time: 64.3 us -> 62.6 us (0.974)
  Pallas kernels: 61 us -> 59.3 us
    pallas_call x1, Pallas kernels: 61 us -> 59.3 us  [body(): pl.pallas_call(functools.partial(kernel, nx, ny, bx, by, reactions), out_...]
where the time goes in v4:
time: 62.6 us; the launch traced here: 62.5 us
  Pallas kernels  59.3 us (95%)
  local copies, waits for them, and re-layouts  2.53 us (4%)
  between operations  0.65 us (1%)
    pallas_call x1, Pallas kernels, body(): pl.pallas_call(functools.partial(kernel, nx, ny, bx, by, reactions), out_...  59.3 us
    unnamed x4, local copies, waits for them, and re-layouts  2.53 us

profile of v4, /device:TPU:1, one launch (start us, length us, event | category | flops | bytes accessed | tf_op | source)
XLA Modules:
  0.0 62.5 jit_solution(13403463740244388559)
XLA Ops:
  0.6 59.3 %shard_map.68 = (f32[4096,256]{1,0:T(8,128)S(1)}, f32[2]{0:T(128)}) custom-call(f32[4096,256]{1,0:T(8,128)} %bitcast.4, f32[6]{0:T(128)} %rates.1, s32[3,6]{1,0:T(4,128)} %bitcast.5, s32[2,3]{1,0:T(2,128)} %box.1, s32[2]{0:T(128)} %truncation.1), custom_call_target="tpu_custom_call" | custom-call | tf_op jit(solution)/shard_map/pallas_call | solution.py:527
  60.0 0.0 copy-start
  60.0 2.0 %copy.9 = f32[32,128,256]{2,1,0:T(8,128)} copy(f32[32,128,256]{2,1,0:T(8,128)S(1)} %bitcast.3) | data formatting | bytes 8388608
  62.0 0.0 copy-done
  62.0 0.5 copy.10
Async XLA Ops:
  60.0 2.0 %copy-start = (f32[2]{0:T(128)S(1)}, f32[2]{0:T(128)}, u32[]{:S(2)}) copy-start(f32[2]{0:T(128)} %get-tuple-element.11) | copy-start | bytes 28

commit v5 on v4

--- a/solution.py
+++ b/solution.py
@@ -42,7 +42,7 @@
     nx, ny, bx, by, reactions,
     density, rates, changes, box, truncation,
     occupancy, summary,
-    p, s, d, parts, movers, shifted_b, plain_b, free_table, box_table,
+    p, s, d, parts, movers, shifted_b, plain_b, self_c, free_table, box_table,
     recv_x, recv_y, recv_c, send_y, send_c, red_near, red_far,
     load_sem, send_sem, recv_sem, nsend_sem, nrecv_sem, fsend_sem, frecv_sem,
 ):
@@ -223,7 +223,6 @@
     rows = lax.broadcasted_iota(jnp.int32, (by, LANES), 0) + anchor_y
     for r in range(reactions):
         shifted_b[r] = evaluate(phi[r][1], (rows - changes[1, r]).astype(jnp.float32))
-        plain_b[r] = evaluate(phi[r][1], rows.astype(jnp.float32))
     y_box = within(rows, 1).astype(jnp.float32)
     for h in range(2):
         inside = y_box * z_box[h]
@@ -388,28 +387,47 @@
             advance_to(k, x, middle)
 
     def self_term():
-        z_factor = [
-            [
-                jnp.where(order[r][2] == 0, jnp.ones_like(z_one[h]), jnp.where(order[r][2] == 1, z_one[h], z_two[h]))
-                for h in range(2)
-            ]
-            for r in range(reactions)
+        def pick(index, values):
+            out = jnp.zeros(index.shape, jnp.float32)
+            for r, value in enumerate(values):
+                out = jnp.where(index == r, value, out)
+            return out
+
+        column = lanes(1)
+        reaction, piece = column & 7, column >> 4
+        along = [
+            tuple(pick(reaction, [phi[r][a][i] for r in range(reactions)]) for i in range(3))
+            for a in range(2)
         ]
-
-        @pl.loop(0, bx)
-        def _(x):
-            factors = along_x(x, False)
-            taken = within(anchor_x + x, 0).astype(jnp.int32)
-            for y0, n in whole:
-                total = [None, None]
-                for r in range(reactions):
-                    along = factors[r] * plain_b[r, pl.ds(y0, n), :]
-                    for h in range(2):
-                        term = along * z_factor[r][h]
-                        total[h] = term if total[h] is None else total[h] + term
+        rate = jnp.where(column < 48, pick(reaction, [rates[r] for r in range(reactions)]), 0.0)
+        plain_b[...] = evaluate(along[1], rows.astype(jnp.float32))
+        row = lax.broadcasted_iota(jnp.int32, (LANES, LANES), 0)
+        for h in range(2):
+            factor = pick(row & 7, [evaluate(phi[r][2], z_float[h]) for r in range(reactions)])
+            coarse = factor.astype(jnp.bfloat16).astype(jnp.float32)
+            factor = jnp.where((row >> 3) & 1 == 0, coarse, factor - coarse)
+            self_c[:, pl.ds(h * LANES, LANES)] = factor.astype(jnp.bfloat16)
+
+        @pl.loop(0, bx // GROUP)
+        def _(group):
+            first = group * GROUP
+            for i in range(GROUP):
+                count = (anchor_x + first + i).astype(jnp.float32)
+                value = (rate * evaluate(along[0], count)) * plain_b[...]
+                high = value.astype(jnp.bfloat16).astype(jnp.float32)
+                rest = value - high
+                middle_part = rest.astype(jnp.bfloat16).astype(jnp.float32)
+                part = jnp.where(piece == 0, high, jnp.where(piece == 1, middle_part, rest - middle_part))
+                parts[pl.ds(i * by, by), pl.ds(0, LANES)] = part.astype(jnp.bfloat16)
+            total = jnp.dot(
+                parts[:, pl.ds(0, LANES)], self_c[...], preferred_element_type=jnp.float32
+            )
+            for i in range(GROUP):
+                taken = within(anchor_x + first + i, 0).astype(jnp.int32)
+                base = pl.multiple_of((first + i) * by, 8)
                 for h in range(2):
-                    base = pl.multiple_of(x * by + y0, 8)
-                    d[h, pl.ds(base, n), :] = 1.0 - total[h] * free_table[taken, h, pl.ds(y0, n), :]
+                    a0 = total[i * by : (i + 1) * by, h * LANES : (h + 1) * LANES]
+                    d[h, pl.ds(base, by), :] = 1.0 - a0 * free_table[taken, h]
 
     scale_own(0)
     self_term()
@@ -543,7 +561,8 @@
             pltpu.VMEM((GROUP * by, 4 * LANES), jnp.bfloat16),
             pltpu.VMEM((len(MOVED), 4 * LANES, 2 * LANES), jnp.bfloat16),
             vmem(reactions, by, LANES),
-            vmem(reactions, by, LANES),
+            vmem(by, LANES),
+            pltpu.VMEM((LANES, 2 * LANES), jnp.bfloat16),
             vmem(2, 2, by, LANES),
             vmem(2, 2, by, LANES),
             vmem(STEPS, 2, 2, 2 * by, LANES),

time: 62.6 us -> 61 us (0.974)
  Pallas kernels: 59.3 us -> 57.8 us
    pallas_call x1, Pallas kernels: 59.3 us -> 57.8 us  [body(): pl.pallas_call(functools.partial(kernel, nx, ny, bx, by, reactions), out_...]
where the time goes in v5:
time: 61 us
  Pallas kernels  57.8 us (95%)
  local copies, waits for them, and re-layouts  2.53 us (4%)
  between operations  0.65 us (1%)
    pallas_call x1, Pallas kernels, body(): pl.pallas_call(functools.partial(kernel, nx, ny, bx, by, reactions), out_...  57.8 us
    unnamed x4, local copies, waits for them, and re-layouts  2.53 us

profile of v5, /device:TPU:1, one launch (start us, length us, event | category | flops | bytes accessed | tf_op | source)
XLA Modules:
  0.0 61.0 jit_solution(1792985717842361866)
XLA Ops:
  0.6 57.8 %shard_map.68 = (f32[4096,256]{1,0:T(8,128)S(1)}, f32[2]{0:T(128)}) custom-call(f32[4096,256]{1,0:T(8,128)} %bitcast.4, f32[6]{0:T(128)} %rates.1, s32[3,6]{1,0:T(4,128)} %bitcast.5, s32[2,3]{1,0:T(2,128)} %box.1, s32[2]{0:T(128)} %truncation.1), custom_call_target="tpu_custom_call" | custom-call | tf_op jit(solution)/shard_map/pallas_call | solution.py:545
  58.5 0.0 copy-start
  58.5 2.0 %copy.9 = f32[32,128,256]{2,1,0:T(8,128)} copy(f32[32,128,256]{2,1,0:T(8,128)S(1)} %bitcast.3) | data formatting | bytes 8388608
  60.5 0.0 copy-done
  60.5 0.5 copy.10
Async XLA Ops:
  58.5 2.0 %copy-start = (f32[2]{0:T(128)S(1)}, f32[2]{0:T(128)}, u32[]{:S(2)}) copy-start(f32[2]{0:T(128)} %get-tuple-element.11) | copy-start | bytes 28
